TPU v7x, 512 devices: a whole 4x8x8 slice. The times are simulated.
512 devices in a mesh: px: 32 (over y, x), py: 16 (over z, core).
Axes of the slice: x: 4, y: 8, z: 8, core: 2. Of those that a mesh axis runs over, the one named last changes fastest.
Arguments:
- node_features: bfloat16 [262144, 192], P(('px', 'py')), may hold values from -6 to 6
- edge_source: int32 [512, 3072], P(('px', 'py')), may hold values from 0 to 767
- edge_target: int32 [512, 3072], P(('px', 'py')), may hold values from 0 to 512, as said below
- halo_send: int32 [512, 64], P(('px', 'py')), may hold values from 0 to 511
- edge_weight_in: bfloat16 [384, 192], replicated, may hold values from -0.3125 to 0.3125
- edge_bias: float32 [192], replicated, may hold values from -4 to 4
- edge_weight_out: bfloat16 [192, 192], replicated, may hold values from -0.4375 to 0.4375
- node_weight_in: bfloat16 [384, 192], replicated, may hold values from -0.3125 to 0.3125
- node_bias: float32 [192], replicated, may hold values from -4 to 4
- node_weight_out: bfloat16 [192, 192], replicated, may hold values from -0.4375 to 0.4375
- cluster_owner: int32 [262144, 1], P(('px', 'py')), may hold values from 0 to 15; in each aligned block of 512 rows (0 to 511, 512 to 1023, ...) at most 64 rows name the same one
- cluster_member: int32 [262144], P(('px', 'py')), may hold values from 0 to 63
- coarse_send: int32 [512, 16], P(('px', 'py')), may hold values from 0 to 63
- coarse_source: int32 [512, 384], P(('px', 'py')), may hold values from 0 to 127
- coarse_target: int32 [512, 384], P(('px', 'py')), may hold values from 0 to 64, as said below
- coarse_edge_in: bfloat16 [384, 192], replicated, may hold values from -0.3125 to 0.3125
- coarse_edge_bias: float32 [192], replicated, may hold values from -4 to 4
- coarse_edge_out: bfloat16 [192, 192], replicated, may hold values from -0.4375 to 0.4375
- coarse_node_in: bfloat16 [384, 192], replicated, may hold values from -0.3125 to 0.3125
- coarse_node_bias: float32 [192], replicated, may hold values from -4 to 4
- coarse_node_out: bfloat16 [192, 192], replicated, may hold values from -0.4375 to 0.4375
Outputs:
- node_updated: bfloat16 [262144, 192], P(('px', 'py'))
- cluster_updated: bfloat16 [32768, 192], P(('px', 'py'))
Inputs may be any that keep to these rules, and one draw needn't show every extreme that they name: `edge_target`: each device's slots hold a target node of that device; padding slots hold 512 and stand only at the end of a device's list; at least three quarters of each device's slots are live and some device has no padding. `coarse_target`: each device's slots hold a target cluster of that device; padding slots hold 64 and stand only at the end of a device's list; at least three quarters of each device's slots are live and some device has no padding. `cluster_owner`: at most 64 nodes of one device have the same owner, and in every draw some device has exactly 64 nodes with one owner.
All inputs are finite; a program needn't handle non-finite values.
Results may differ from a plain program's by a relative error of at most 0.014.
Values may be sent and summed in bfloat16 or wider, within the bound.
No kernel may reach another device: no remote copies, remote signals or barrier semaphores. Data moves between devices by JAX's collectives and lax.ppermute only.
A program may use at most 64 MiB of HBM per device.

v0:
```python
import math

import jax
import jax.numpy as jnp
from jax import lax
from jax.sharding import PartitionSpec as P

CLUST_DEV = 64


def padded_2(block, sides, width):
    for axis, dim in sides:
        count = lax.axis_size(axis)
        forward = [(i, i + 1) for i in range(count - 1)]
        backward = [(target, source) for source, target in forward]
        low = lax.ppermute(
            lax.slice_in_dim(block, block.shape[dim] - width, None, axis=dim), axis, forward
        )
        high = lax.ppermute(lax.slice_in_dim(block, 0, width, axis=dim), axis, backward)
        block = jnp.concatenate([low, block, high], axis=dim)
    return block


def normed(values):
    center = values - jnp.mean(values, axis=-1, keepdims=True)
    return center * lax.rsqrt(jnp.mean(center * center, axis=-1, keepdims=True) + 1e-05)


def rim_rows(padded):
    return (padded[0, 1], padded[2, 1], padded[1, 0], padded[1, 2])


def pick_rows(row_ids, table):
    selector = (row_ids[:, None] == lax.broadcasted_iota(jnp.int32, (1, table.shape[0]), 1)).astype(
        jnp.bfloat16
    )
    return jnp.dot(selector, table, preferred_element_type=jnp.float32).astype(jnp.bfloat16)


def one_round(features, lookup_table, sources, targets, weights):
    weight_in, bias, weight_out, node_in, node_bias, node_out = weights
    amount = features.shape[0]
    edge_total = sources.shape[0]
    block_rows = math.gcd(edge_total, 768)
    groups = edge_total // block_rows

    def add_block(totals, pieces):
        block_sources, block_targets = pieces
        paired = jnp.concatenate(
            [pick_rows(block_sources, lookup_table), pick_rows(block_targets, features)], axis=1
        )
        hidden = jax.nn.silu(
            jnp.dot(paired, weight_in, preferred_element_type=jnp.float32) + bias
        ).astype(jnp.bfloat16)
        message = normed(jnp.dot(hidden, weight_out, preferred_element_type=jnp.float32))
        upper = message.astype(jnp.bfloat16)
        lower = (message - upper.astype(jnp.float32)).astype(jnp.bfloat16)
        spread = (lax.broadcasted_iota(jnp.int32, (amount, 1), 0) == block_targets[None, :]).astype(
            jnp.bfloat16
        )
        added = jnp.dot(spread, upper, preferred_element_type=jnp.float32) + jnp.dot(
            spread, lower, preferred_element_type=jnp.float32
        )
        return (totals + added, None)

    totals, unused = lax.scan(
        add_block,
        jnp.zeros((amount, features.shape[1]), jnp.float32),
        (sources.reshape(groups, block_rows), targets.reshape(groups, block_rows)),
    )
    joined = jnp.concatenate([features, totals.astype(jnp.bfloat16)], axis=1)
    node_hidden = jax.nn.silu(
        jnp.dot(joined, node_in, preferred_element_type=jnp.float32) + node_bias
    ).astype(jnp.bfloat16)
    return (
        features.astype(jnp.float32)
        + normed(jnp.dot(node_hidden, node_out, preferred_element_type=jnp.float32))
    ).astype(jnp.bfloat16)


def body(
    node_features,
    edge_source,
    edge_target,
    halo_send,
    edge_weight_in,
    edge_bias,
    edge_weight_out,
    node_weight_in,
    node_bias,
    node_weight_out,
    cluster_owner,
    cluster_member,
    coarse_send,
    coarse_source,
    coarse_target,
    coarse_edge_in,
    coarse_edge_bias,
    coarse_edge_out,
    coarse_node_in,
    coarse_node_bias,
    coarse_node_out,
):
    shared_nodes = pick_rows(halo_send[0], node_features)
    padded = padded_2(shared_nodes[None, None], (("px", 0), ("py", 1)), 1)
    lookup_table = jnp.concatenate((node_features,) + rim_rows(padded), axis=0)
    node_updated = one_round(
        node_features,
        lookup_table,
        edge_source[0],
        edge_target[0],
        (edge_weight_in, edge_bias, edge_weight_out, node_weight_in, node_bias, node_weight_out),
    )
    owners = cluster_owner[:, 0]
    owner_count = lax.axis_size("py")
    position = owners * CLUST_DEV + cluster_member
    member_of = (
        lax.broadcasted_iota(jnp.int32, (owner_count * CLUST_DEV, 1), 0) == position[None, :]
    ).astype(jnp.bfloat16)
    pooled = jnp.dot(member_of, node_updated, preferred_element_type=jnp.float32)
    counts = jnp.sum(member_of.astype(jnp.float32), axis=1)
    pooled, counts = (
        lax.psum_scatter(pooled.astype(jnp.bfloat16), "py", scatter_dimension=0, tiled=True).astype(
            jnp.float32
        ),
        lax.psum_scatter(counts.astype(jnp.bfloat16), "py", scatter_dimension=0, tiled=True).astype(
            jnp.float32
        ),
    )
    coarse = (pooled / jnp.maximum(counts, 1.0)[:, None]).astype(jnp.bfloat16)
    coarse_shared = pick_rows(coarse_send[0], coarse)
    coarse_padded = padded_2(coarse_shared[None, None], (("px", 0), ("py", 1)), 1)
    coarse_table = jnp.concatenate((coarse,) + rim_rows(coarse_padded), axis=0)
    cluster_updated = one_round(
        coarse,
        coarse_table,
        coarse_source[0],
        coarse_target[0],
        (
            coarse_edge_in,
            coarse_edge_bias,
            coarse_edge_out,
            coarse_node_in,
            coarse_node_bias,
            coarse_node_out,
        ),
    )
    return (node_updated, cluster_updated)


def solution(mesh):
    placed = (
        P(("px", "py"), None),
        P(("px", "py"), None),
        P(("px", "py"), None),
        P(("px", "py"), None),
        P(),
        P(),
        P(),
        P(),
        P(),
        P(),
        P(("px", "py"), None),
        P(("px", "py")),
        P(("px", "py"), None),
        P(("px", "py"), None),
        P(("px", "py"), None),
        P(),
        P(),
        P(),
        P(),
        P(),
        P(),
    )
    return jax.shard_map(
        body,
        mesh=mesh,
        in_specs=placed,
        out_specs=(P(("px", "py"), None), P(("px", "py"), None)),
        check_vma=False,
    )
```

profile of v0, /device:TPU:31, one launch (start us, length us, event | category | flops | bytes accessed | tf_op | source)
XLA Modules:
  0.0 140.5 jit_solution(761919122915345740)
XLA Ops:
  7.3 1.2 fusion.33
  8.4 4.5 %collective-permute-start = (bf16[1,1,64,192]{3,2,1,0:T(8,128)(2,1)S(1)}, bf16[1,1,64,192]{3,2,1,0:T(8,128)(2,1)S(1)}, u32[]{:S(2)}, u32[]{:S(2)}) collective-permute-start(bf16[1,1,64,192]{3,2,1,0:T(8,128)(2,1)S(1)} %fusion.33), channel_id=1, source_target_pairs={{0,16},{16,32},{32,48},{48,64},{64,80},{80,96},{96,112},{112,128},... | collective-permute-start | bytes 73736 | tf_op jit(solution)/shard_map/ppermute | solution.py:16
  12.9 1.9 %collective-permute-start.1 = (bf16[1,1,64,192]{3,2,1,0:T(8,128)(2,1)S(1)}, bf16[1,1,64,192]{3,2,1,0:T(8,128)(2,1)S(1)}, u32[]{:S(2)}, u32[]{:S(2)}) collective-permute-start(bf16[1,1,64,192]{3,2,1,0:T(8,128)(2,1)S(1)} %fusion.33), channel_id=1, source_target_pairs={{16,0},{32,16},{48,32},{64,48},{80,64},{96,80},{112,96},{128,112},... | collective-permute-start | bytes 73736 | tf_op jit(solution)/shard_map/ppermute | solution.py:19
  14.8 1.1 copy.25
  16.0 0.5 broadcast.137
  16.5 0.7 reduce.13
  17.2 0.7 reduce.14
  18.0 2.9 %collective-permute-done.1 = bf16[1,1,64,192]{3,2,1,0:T(8,128)(2,1)S(1)} collective-permute-done((bf16[1,1,64,192]{3,2,1,0:T(8,128)(2,1)S(1)}, bf16[1,1,64,192]{3,2,1,0:T(8,128)(2,1)S(1)}, u32[]{:S(2)}, u32[]{:S(2)}) %collective-permute-start.1) | collective-permute-done | bytes 24608 | tf_op jit(solution)/shard_map/ppermute | solution.py:19
  20.9 6.0 %collective-permute-start.2 = (bf16[3,1,64,192]{3,2,1,0:T(8,128)(2,1)S(1)}, bf16[3,1,64,192]{3,2,1,0:T(8,128)(2,1)S(1)}, u32[]{:S(2)}, u32[]{:S(2)}) collective-permute-start(bf16[3,1,64,192]{3,2,1,0:T(8,128)(2,1)S(1)} %pad_maximum_fusion), channel_id=1, source_target_pairs={{0,1},{1,2},{2,3},{3,4},{4,5},{5,6},{6,7},{7,8},{8,9},{9,10},{10,1... | collective-permute-start | bytes 221192 | tf_op jit(solution)/shard_map/ppermute | solution.py:16
  26.9 1.9 %collective-permute-start.3 = (bf16[3,1,64,192]{3,2,1,0:T(8,128)(2,1)S(1)}, bf16[3,1,64,192]{3,2,1,0:T(8,128)(2,1)S(1)}, u32[]{:S(2)}, u32[]{:S(2)}) collective-permute-start(bf16[3,1,64,192]{3,2,1,0:T(8,128)(2,1)S(1)} %pad_maximum_fusion), channel_id=1, source_target_pairs={{1,0},{2,1},{3,2},{4,3},{5,4},{6,5},{7,6},{8,7},{9,8},{10,9},{11,1... | collective-permute-start | bytes 221192 | tf_op jit(solution)/shard_map/ppermute | solution.py:19
  28.9 4.0 %collective-permute-done.3 = bf16[3,1,64,192]{3,2,1,0:T(8,128)(2,1)S(1)} collective-permute-done((bf16[3,1,64,192]{3,2,1,0:T(8,128)(2,1)S(1)}, bf16[3,1,64,192]{3,2,1,0:T(8,128)(2,1)S(1)}, u32[]{:S(2)}, u32[]{:S(2)}) %collective-permute-start.3) | collective-permute-done | bytes 73760 | tf_op jit(solution)/shard_map/ppermute | solution.py:19
  32.9 12.6 %while.3 = (s32[]{:T(128)}, f32[512,192]{0,1:T(8,128)S(1)}, s32[4,768]{1,0:T(4,128)S(1)}, s32[4,768]{1,0:T(4,128)S(1)}, bf16[768,192]{1,0:T(8,128)(2,1)S(1)}, /*...) while((s32[]{:T(128)}, f32[512,192]{0,1:T(8,128)S(1)}, ...), condition=%wide.region_3.4_spmd.clone, body=%wide.region_0.3_spmd.clone.sunk | while | flops 855687936 | bytes 5883771 | solution.py:66
  32.9 0.6 fusion.131
  33.5 0.7 fusion.132
  34.2 0.6 fusion.133
  34.9 0.5 fusion.134
  35.4 0.6 fusion.135
  36.1 0.6 fusion.131
  36.6 0.7 fusion.132
  37.4 0.6 fusion.133
  38.1 0.5 fusion.134
  38.6 0.6 fusion.135
  39.2 0.6 fusion.131
  39.8 0.7 fusion.132
  40.5 0.6 fusion.133
  41.2 0.5 fusion.134
  41.7 0.6 fusion.135
  42.4 0.6 fusion.131
  42.9 0.7 fusion.132
  43.7 0.6 fusion.133
  44.4 0.5 fusion.134
  44.9 0.6 fusion.135
  45.5 0.8 copy-done.13
  46.4 0.5 fusion.92
  47.1 1.3 fusion.31
  48.5 1.3 dynamic-slice
  50.7 27.1 %all-reduce = bf16[1024]{0:T(1024)(128)(2,1)S(1)} all-reduce(bf16[1024]{0:T(1024)(128)(2,1)S(1)} %fusion.35), channel_id=3, replica_groups=mesh['px'=32,'py'=16] {'py'}, use_global_device_ids=true, to_apply=%region_8.9.clone | all-reduce | flops 1024 | bytes 4096
  77.9 29.4 %reduce-scatter.2.cloned.1.call-done = bf16[64,192]{1,0:T(8,128)(2,1)} async-done(((bf16[1024,192]{1,0:T(8,128)(2,1)}), bf16[64,192]{1,0:T(8,128)(2,1)}) %reduce-scatter.2.cloned.1.call-update) | async-done | bytes 24592 | tf_op jit(solution)/shard_map/reduce_scatter | solution.py:123
  107.3 0.8 constant_dynamic-update-slice_fusion.5
  108.3 4.2 %collective-permute-start.4 = (bf16[1,1,16,192]{3,2,1,0:T(8,128)(2,1)S(1)}, bf16[1,1,16,192]{3,2,1,0:T(8,128)(2,1)S(1)}, u32[]{:S(2)}, u32[]{:S(2)}) collective-permute-start(bf16[1,1,16,192]{3,2,1,0:T(8,128)(2,1)S(1)} %fusion.34), channel_id=1, source_target_pairs={{0,16},{16,32},{32,48},{48,64},{64,80},{80,96},{96,112},{112,128},... | collective-permute-start | bytes 18440 | tf_op jit(solution)/shard_map/ppermute | solution.py:16
  112.6 1.9 %collective-permute-start.5 = (bf16[1,1,16,192]{3,2,1,0:T(8,128)(2,1)S(1)}, bf16[1,1,16,192]{3,2,1,0:T(8,128)(2,1)S(1)}, u32[]{:S(2)}, u32[]{:S(2)}) collective-permute-start(bf16[1,1,16,192]{3,2,1,0:T(8,128)(2,1)S(1)} %fusion.34), channel_id=1, source_target_pairs={{16,0},{32,16},{48,32},{64,48},{80,64},{96,80},{112,96},{128,112},... | collective-permute-start | bytes 18440 | tf_op jit(solution)/shard_map/ppermute | solution.py:19
  114.8 5.5 %collective-permute-done.5 = bf16[1,1,16,192]{3,2,1,0:T(8,128)(2,1)S(1)} collective-permute-done((bf16[1,1,16,192]{3,2,1,0:T(8,128)(2,1)S(1)}, bf16[1,1,16,192]{3,2,1,0:T(8,128)(2,1)S(1)}, u32[]{:S(2)}, u32[]{:S(2)}) %collective-permute-start.5) | collective-permute-done | bytes 6176 | tf_op jit(solution)/shard_map/ppermute | solution.py:19
  120.3 5.0 %collective-permute-start.6 = (bf16[3,1,16,192]{3,2,1,0:T(8,128)(2,1)S(1)}, bf16[3,1,16,192]{3,2,1,0:T(8,128)(2,1)S(1)}, u32[]{:S(2)}, u32[]{:S(2)}) collective-permute-start(bf16[3,1,16,192]{3,2,1,0:T(8,128)(2,1)S(1)} %pad_maximum_fusion.1), channel_id=1, source_target_pairs={{0,1},{1,2},{2,3},{3,4},{4,5},{5,6},{6,7},{7,8},{8,9},{9,10},{10,1... | collective-permute-start | bytes 55304 | tf_op jit(solution)/shard_map/ppermute | solution.py:16
  125.3 3.2 %collective-permute-start.7 = (bf16[3,1,16,192]{3,2,1,0:T(8,128)(2,1)S(1)}, bf16[3,1,16,192]{3,2,1,0:T(8,128)(2,1)S(1)}, u32[]{:S(2)}, u32[]{:S(2)}) collective-permute-start(bf16[3,1,16,192]{3,2,1,0:T(8,128)(2,1)S(1)} %pad_maximum_fusion.1), channel_id=1, source_target_pairs={{1,0},{2,1},{3,2},{4,3},{5,4},{6,5},{7,6},{8,7},{9,8},{10,9},{11,1... | collective-permute-start | bytes 55304 | tf_op jit(solution)/shard_map/ppermute | solution.py:19
  128.5 1.9 %collective-permute-done.7 = bf16[3,1,16,192]{3,2,1,0:T(8,128)(2,1)S(1)} collective-permute-done((bf16[3,1,16,192]{3,2,1,0:T(8,128)(2,1)S(1)}, bf16[3,1,16,192]{3,2,1,0:T(8,128)(2,1)S(1)}, u32[]{:S(2)}, u32[]{:S(2)}) %collective-permute-start.7) | collective-permute-done | bytes 18464 | tf_op jit(solution)/shard_map/ppermute | solution.py:19
  130.8 0.5 fusion.95
  132.3 0.4 fusion.98
  132.9 0.7 add_convert_fusion.1
  (99 shorter events, 3.3 us)
Async XLA Ops:
  7.2 38.3 %copy-start = (bf16[384,192]{0,1:T(8,128)(2,1)S(1)}, bf16[384,192]{0,1:T(8,128)(2,1)}, u32[]{:S(2)}) copy-start(bf16[384,192]{0,1:T(8,128)(2,1)} %param.30) | copy-start | bytes 442372
  7.2 8.7 %copy-start.6 = (s32[512,1]{0,1:T(1,128)S(1)}, s32[512,1]{0,1:T(1,128)}, u32[]{:S(2)}) copy-start(s32[512,1]{0,1:T(1,128)} %param.33) | copy-start | bytes 6148
  7.2 100.1 %reduce-scatter.2.cloned.1.call-start = ((), (), s32[]{:S(2)}) async-start(), calls=%async_computation.1 | async-start | bytes 557056 | tf_op jit(solution)/shard_map/reduce_scatter | solution.py:123
  7.2 9.3 %copy-start.3 = (s32[1,3072]{1,0:T(1,128)S(1)}, s32[1,3072]{1,0:T(1,128)}, u32[]{:S(2)}) copy-start(s32[1,3072]{1,0:T(1,128)} %param.25) | copy-start | bytes 36868
  7.2 10.0 %copy-start.4 = (s32[1,3072]{1,0:T(1,128)S(1)}, s32[1,3072]{1,0:T(1,128)}, u32[]{:S(2)}) copy-start(s32[1,3072]{1,0:T(1,128)} %param.24) | copy-start | bytes 36868
  8.4 9.5 %copy-start.5 = (s32[512]{0:T(512)S(1)}, s32[512]{0:T(512)}, u32[]{:S(2)}) copy-start(s32[512]{0:T(512)} %param.34) | copy-start | bytes 6148
  8.4 9.5 %collective-permute-start = (bf16[1,1,64,192]{3,2,1,0:T(8,128)(2,1)S(1)}, bf16[1,1,64,192]{3,2,1,0:T(8,128)(2,1)S(1)}, u32[]{:S(2)}, u32[]{:S(2)}) collective-permute-start(bf16[1,1,64,192]{3,2,1,0:T(8,128)(2,1)S(1)} %fusion.33), channel_id=1, source_target_pairs={{0,16},{16,32},{32,48},{48,64},{64,80},{80,96},{96,112},{112,128},... | collective-permute-start | bytes 73736 | tf_op jit(solution)/shard_map/ppermute | solution.py:16
  12.9 8.0 %collective-permute-start.1 = (bf16[1,1,64,192]{3,2,1,0:T(8,128)(2,1)S(1)}, bf16[1,1,64,192]{3,2,1,0:T(8,128)(2,1)S(1)}, u32[]{:S(2)}, u32[]{:S(2)}) collective-permute-start(bf16[1,1,64,192]{3,2,1,0:T(8,128)(2,1)S(1)} %fusion.33), channel_id=1, source_target_pairs={{16,0},{32,16},{48,32},{64,48},{80,64},{96,80},{112,96},{128,112},... | collective-permute-start | bytes 73736 | tf_op jit(solution)/shard_map/ppermute | solution.py:19
  15.9 16.9 %copy-start.1 = (bf16[512,192]{0,1:T(8,128)(2,1)S(1)}, bf16[512,192]{0,1:T(8,128)(2,1)}, u32[]{:S(2)}) copy-start(bf16[512,192]{0,1:T(8,128)(2,1)} %param.23) | copy-start | bytes 589828
  15.9 16.9 %copy-start.9 = (bf16[384,192]{0,1:T(8,128)(2,1)S(1)}, bf16[384,192]{0,1:T(8,128)(2,1)}, u32[]{:S(2)}) copy-start(bf16[384,192]{0,1:T(8,128)(2,1)} %param.27) | copy-start | bytes 442372
  15.9 16.9 %copy-start.12 = (bf16[192,192]{1,0:T(8,128)(2,1)S(1)}, bf16[192,192]{1,0:T(8,128)(2,1)}, u32[]{:S(2)}) copy-start(bf16[192,192]{1,0:T(8,128)(2,1)} %param.29) | copy-start | bytes 221188
  16.0 16.9 %copy-start.16 = (f32[192]{0:T(256)S(1)}, f32[192]{0:T(256)}, u32[]{:S(2)}) copy-start(f32[192]{0:T(256)} %param.28) | copy-start | bytes 2308
  20.9 8.0 %collective-permute-start.2 = (bf16[3,1,64,192]{3,2,1,0:T(8,128)(2,1)S(1)}, bf16[3,1,64,192]{3,2,1,0:T(8,128)(2,1)S(1)}, u32[]{:S(2)}, u32[]{:S(2)}) collective-permute-start(bf16[3,1,64,192]{3,2,1,0:T(8,128)(2,1)S(1)} %pad_maximum_fusion), channel_id=1, source_target_pairs={{0,1},{1,2},{2,3},{3,4},{4,5},{5,6},{6,7},{7,8},{8,9},{9,10},{10,1... | collective-permute-start | bytes 221192 | tf_op jit(solution)/shard_map/ppermute | solution.py:16
  26.9 5.9 %collective-permute-start.3 = (bf16[3,1,64,192]{3,2,1,0:T(8,128)(2,1)S(1)}, bf16[3,1,64,192]{3,2,1,0:T(8,128)(2,1)S(1)}, u32[]{:S(2)}, u32[]{:S(2)}) collective-permute-start(bf16[3,1,64,192]{3,2,1,0:T(8,128)(2,1)S(1)} %pad_maximum_fusion), channel_id=1, source_target_pairs={{1,0},{2,1},{3,2},{4,3},{5,4},{6,5},{7,6},{8,7},{9,8},{10,9},{11,1... | collective-permute-start | bytes 221192 | tf_op jit(solution)/shard_map/ppermute | solution.py:19
  45.5 0.9 copy-start.13
  45.5 0.9 copy-start.17
  47.1 1.3 copy-start.2
  47.1 1.4 copy-start.7
  47.1 1.4 copy-start.8
  48.4 59.7 %copy-start.20 = (s32[1,16]{1,0:T(1,128)S(1)}, s32[1,16]{1,0:T(1,128)}, u32[]{:S(2)}) copy-start(s32[1,16]{1,0:T(1,128)} %param.35) | copy-start | bytes 196
  48.4 82.4 %copy-start.10 = (bf16[384,192]{0,1:T(8,128)(2,1)S(1)}, bf16[384,192]{0,1:T(8,128)(2,1)}, u32[]{:S(2)}) copy-start(bf16[384,192]{0,1:T(8,128)(2,1)} %param.38) | copy-start | bytes 442372
  48.4 82.4 %copy-start.14 = (bf16[192,192]{1,0:T(8,128)(2,1)S(1)}, bf16[192,192]{1,0:T(8,128)(2,1)}, u32[]{:S(2)}) copy-start(bf16[192,192]{1,0:T(8,128)(2,1)} %param.40) | copy-start | bytes 221188
  48.4 82.4 %copy-start.18 = (f32[192]{0:T(256)S(1)}, f32[192]{0:T(256)}, u32[]{:S(2)}) copy-start(f32[192]{0:T(256)} %param.39) | copy-start | bytes 2308
  108.3 6.5 %collective-permute-start.4 = (bf16[1,1,16,192]{3,2,1,0:T(8,128)(2,1)S(1)}, bf16[1,1,16,192]{3,2,1,0:T(8,128)(2,1)S(1)}, u32[]{:S(2)}, u32[]{:S(2)}) collective-permute-start(bf16[1,1,16,192]{3,2,1,0:T(8,128)(2,1)S(1)} %fusion.34), channel_id=1, source_target_pairs={{0,16},{16,32},{32,48},{48,64},{64,80},{80,96},{96,112},{112,128},... | collective-permute-start | bytes 18440 | tf_op jit(solution)/shard_map/ppermute | solution.py:16
  112.6 7.7 %collective-permute-start.5 = (bf16[1,1,16,192]{3,2,1,0:T(8,128)(2,1)S(1)}, bf16[1,1,16,192]{3,2,1,0:T(8,128)(2,1)S(1)}, u32[]{:S(2)}, u32[]{:S(2)}) collective-permute-start(bf16[1,1,16,192]{3,2,1,0:T(8,128)(2,1)S(1)} %fusion.34), channel_id=1, source_target_pairs={{16,0},{32,16},{48,32},{64,48},{80,64},{96,80},{112,96},{128,112},... | collective-permute-start | bytes 18440 | tf_op jit(solution)/shard_map/ppermute | solution.py:19
  120.3 8.2 %collective-permute-start.6 = (bf16[3,1,16,192]{3,2,1,0:T(8,128)(2,1)S(1)}, bf16[3,1,16,192]{3,2,1,0:T(8,128)(2,1)S(1)}, u32[]{:S(2)}, u32[]{:S(2)}) collective-permute-start(bf16[3,1,16,192]{3,2,1,0:T(8,128)(2,1)S(1)} %pad_maximum_fusion.1), channel_id=1, source_target_pairs={{0,1},{1,2},{2,3},{3,4},{4,5},{5,6},{6,7},{7,8},{8,9},{9,10},{10,1... | collective-permute-start | bytes 55304 | tf_op jit(solution)/shard_map/ppermute | solution.py:16
  125.3 5.1 %collective-permute-start.7 = (bf16[3,1,16,192]{3,2,1,0:T(8,128)(2,1)S(1)}, bf16[3,1,16,192]{3,2,1,0:T(8,128)(2,1)S(1)}, u32[]{:S(2)}, u32[]{:S(2)}) collective-permute-start(bf16[3,1,16,192]{3,2,1,0:T(8,128)(2,1)S(1)} %pad_maximum_fusion.1), channel_id=1, source_target_pairs={{1,0},{2,1},{3,2},{4,3},{5,4},{6,5},{7,6},{8,7},{9,8},{10,9},{11,1... | collective-permute-start | bytes 55304 | tf_op jit(solution)/shard_map/ppermute | solution.py:19
  131.3 0.9 copy-start.11
  131.3 1.0 copy-start.15
  131.3 0.9 copy-start.19
Sparse Core Ops, SparseCore 0:
  48.5 58.6 reduce-scatter.1
where the time goes:
time: 141 us; the launch traced here: 140 us
  waiting for transfers between devices  43.7 us (31%)
  starting transfers between devices  28.7 us (20%)
  blocking collectives  27.1 us (19%)
  matrix products  16.9 us (12%)
  between operations  15.2 us (11%)
  local copies, waits for them, and re-layouts  4.44 us (3%)
  other arithmetic  4.15 us (3%)
    reduce_scatter x1, waiting for transfers between devices, body(): lax.psum_scatter(pooled.astype(jnp.bfloat16), 'py', scatter_dimension=0,...  29.4 us
    unnamed x1, blocking collectives  27.1 us
    ppermute x4, starting transfers between devices, padded_2(): lax.ppermute(lax.slice_in_dim(block, block.shape[dim] - width, None, axis...  19.7 us
    ppermute x4, waiting for transfers between devices, padded_2(): lax.ppermute(lax.slice_in_dim(block, 0, width, axis=dim), axis, backward)  14.3 us
    ppermute x4, starting transfers between devices, padded_2(): lax.ppermute(lax.slice_in_dim(block, 0, width, axis=dim), axis, backward)  8.91 us
    dot_general x12, matrix products, pick_rows(): jnp.dot(selector, table, preferred_element_type=jnp.float32)  7.18 us
    unnamed x52, local copies, waits for them, and re-layouts  4.31 us
  transfers between devices with their start and end apart: 9, of which 5 were waited for; matrix products, arithmetic and copies ran while one was open for 4% of the time, Pallas kernels for 0%

commit v1 on v0

v1 whole, which is shorter than its diff:
```python
import jax
import jax.numpy as jnp
from jax import lax
from jax.experimental import pallas as pl
from jax.experimental.pallas import tpu as pltpu
from jax.sharding import PartitionSpec as P

WIDTH = 192
CLUST_DEV = 64
OWNERS = 16
BLOCK = 512
F32, BF16, I32 = jnp.float32, jnp.bfloat16, jnp.int32


def nn(a, b):
    return jnp.dot(a, b, preferred_element_type=F32)


def nt(a, b):
    return lax.dot_general(a, b, (((1,), (1,)), ((), ())), preferred_element_type=F32)


def one_hot(ids, count):
    n = ids.shape[1]
    pieces = []
    for start in range(0, count, 256):
        rows = min(256, count - start)
        row = lax.broadcasted_iota(I32, (rows, n), 0).astype(F32).astype(BF16)
        here = (ids - start).astype(F32).astype(BF16)
        pieces.append(jnp.where(row == here, 1.0, 0.0).astype(BF16))
    return pieces[0] if len(pieces) == 1 else jnp.concatenate(pieces, axis=0)


def half_silu(half):
    return half * jnp.tanh(half) + half


def normed(values):
    center = values - jnp.mean(values, axis=0, keepdims=True)
    return center * lax.rsqrt(jnp.mean(center * center, axis=0, keepdims=True) + 1e-05)


def column(row, count):
    at = lax.broadcasted_iota(I32, (count, count), 0) == lax.broadcasted_iota(
        I32, (count, count), 1
    )
    return jnp.sum(jnp.where(at, row.astype(F32), 0.0), axis=1, keepdims=True).astype(I32)


def pick(send, table):
    count, total = send.shape[1], table.shape[1]
    ids = column(send, count)
    chosen = jnp.where(
        lax.broadcasted_iota(I32, (count, total), 1) == ids, 1.0, 0.0
    ).astype(BF16)
    return nt(chosen, table).astype(BF16)


def inside_flags():
    i, j = lax.axis_index("px"), lax.axis_index("py")
    return (i > 0, i < lax.axis_size("px") - 1, j > 0, j < lax.axis_size("py") - 1)


def halo_rows(refs):
    rows = []
    for ref, inside in zip(refs, inside_flags()):
        rows.append(jnp.where(inside, ref[...].astype(F32), 0.0).astype(BF16))
    return jnp.concatenate(rows, axis=0)


def pick_kernel(send_ref, table_ref, out_ref):
    out_ref[...] = pick(send_ref[...], table_ref[...])


def node_stage(features, incoming, node_in, node_bias, node_out):
    joined = jnp.concatenate([features, incoming.astype(BF16)], axis=0)
    hidden = half_silu(0.5 * (nn(node_in, joined) + node_bias)).astype(BF16)
    return features.astype(F32) + normed(nn(node_out, hidden))


def fine_kernel(
    feat_ref,
    h0,
    h1,
    h2,
    h3,
    src_ref,
    tgt_ref,
    win_ref,
    bias_ref,
    wout_ref,
    nin_ref,
    nbias_ref,
    nout_ref,
    owner_ref,
    member_ref,
    updated_ref,
    payload_ref,
    picks_ref,
    totals_ref,
):
    nodes = feat_ref.shape[1]
    features = feat_ref[...]
    w_top, w_bot = win_ref[:, :WIDTH], win_ref[:, WIDTH:]
    rim = halo_rows((h0, h1, h2, h3))
    lookups = nodes + rim.shape[0]
    picks_ref[:, :nodes] = (0.5 * nn(w_top, features)).astype(BF16)
    picks_ref[:, nodes:lookups] = (0.5 * nt(w_top, rim)).astype(BF16)
    picks_ref[:, lookups:] = (0.5 * nn(w_bot, features)).astype(BF16)
    bias = 0.5 * bias_ref[...]
    w_out = wout_ref[...].astype(F32).T.astype(BF16)
    totals_ref[...] = jnp.zeros_like(totals_ref)

    def block(step, carry):
        at = pl.ds(pl.multiple_of(step * BLOCK, BLOCK), BLOCK)
        from_source = one_hot(src_ref[:, at], lookups)
        to_target = one_hot(tgt_ref[:, at], nodes)
        half = nn(picks_ref[:, :lookups], from_source) + nn(picks_ref[:, lookups:], to_target)
        hidden = half_silu(half + bias).astype(BF16)
        message = normed(nn(w_out, hidden)).astype(BF16)
        totals_ref[...] += nt(message, to_target)
        return carry

    lax.fori_loop(0, src_ref.shape[1] // BLOCK, block, 0, unroll=True)

    n_out = nout_ref[...].astype(F32).T.astype(BF16)
    updated = node_stage(features, totals_ref[...], nin_ref[...], nbias_ref[...], n_out)
    updated = updated.astype(BF16)
    updated_ref[...] = updated

    position = owner_ref[...] * CLUST_DEV + member_ref[...]
    counted = jnp.concatenate([updated, jnp.ones((16, nodes), BF16)], axis=0)
    for pair in range(OWNERS // 2):
        member_of = jnp.where(
            lax.broadcasted_iota(I32, (2 * CLUST_DEV, nodes), 0) + pair * 2 * CLUST_DEV
            == position,
            1.0,
            0.0,
        ).astype(BF16)
        pooled = nt(counted, member_of)
        half = WIDTH // 2
        top, low, count = pooled[:half], pooled[half:WIDTH], pooled[WIDTH : WIDTH + 8]
        left = lax.broadcasted_iota(I32, (half, 2 * CLUST_DEV), 1) < CLUST_DEV
        payload_ref[2 * pair, :half, :] = jnp.where(
            left, top, pltpu.roll(low, CLUST_DEV, 1)
        ).astype(BF16)
        payload_ref[2 * pair, half:, :] = count.astype(BF16)
        payload_ref[2 * pair + 1, :half, :] = jnp.where(
            left, pltpu.roll(top, CLUST_DEV, 1), low
        ).astype(BF16)
        payload_ref[2 * pair + 1, half:, :] = pltpu.roll(count, CLUST_DEV, 1).astype(BF16)


def coarse_kernel(parts_ref, send_ref, coarse_ref, shared_ref):
    total = jnp.sum(parts_ref[...].astype(F32), axis=0)
    half = WIDTH // 2
    sums = jnp.concatenate([total[:half], pltpu.roll(total[:half], CLUST_DEV, 1)], axis=0)
    counts = total[half : half + 1]
    coarse = (sums / jnp.maximum(counts, 1.0)).astype(BF16)[:, :CLUST_DEV]
    coarse_ref[...] = coarse
    shared_ref[...] = pick(send_ref[...], coarse)


def level3_kernel(
    feat_ref,
    h0,
    h1,
    h2,
    h3,
    src_ref,
    tgt_ref,
    win_ref,
    bias_ref,
    wout_ref,
    nin_ref,
    nbias_ref,
    nout_ref,
    updated_ref,
):
    nodes = feat_ref.shape[1]
    features = feat_ref[...]
    w_top, w_bot = win_ref[:, :WIDTH], win_ref[:, WIDTH:]
    rim = halo_rows((h0, h1, h2, h3))
    lookups = nodes + rim.shape[0]
    from_source = one_hot(src_ref[...], lookups)
    to_target = one_hot(tgt_ref[...], nodes)
    half = (
        nn((0.5 * nn(w_top, features)).astype(BF16), from_source[:nodes])
        + nn((0.5 * nt(w_top, rim)).astype(BF16), from_source[nodes:])
        + nn((0.5 * nn(w_bot, features)).astype(BF16), to_target)
    )
    hidden = half_silu(half + 0.5 * bias_ref[...]).astype(BF16)
    w_out = wout_ref[...].astype(F32).T.astype(BF16)
    message = normed(nn(w_out, hidden)).astype(BF16)
    totals = nt(message, to_target)
    n_out = nout_ref[...].astype(F32).T.astype(BF16)
    updated = node_stage(features, totals, nin_ref[...], nbias_ref[...], n_out)
    wide = jnp.concatenate([updated, jnp.zeros_like(updated)], axis=1)
    updated_ref[...] = wide.T[:nodes].astype(BF16)


def exchange(shared):
    found = []
    for axis in ("px", "py"):
        count = lax.axis_size(axis)
        ahead = [(k, (k + 1) % count) for k in range(count)]
        found.append(lax.ppermute(shared, axis, ahead))
        found.append(lax.ppermute(shared, axis, [(b, a) for a, b in ahead]))
    return found


def call(kernel, outs, scratch, *args):
    return pl.pallas_call(
        kernel,
        out_shape=[jax.ShapeDtypeStruct(shape, BF16) for shape in outs],
        scratch_shapes=scratch,
        name=kernel.__name__,
    )(*args)


def body(
    node_features,
    edge_source,
    edge_target,
    halo_send,
    edge_weight_in,
    edge_bias,
    edge_weight_out,
    node_weight_in,
    node_bias,
    node_weight_out,
    cluster_owner,
    cluster_member,
    coarse_send,
    coarse_source,
    coarse_target,
    coarse_edge_in,
    coarse_edge_bias,
    coarse_edge_out,
    coarse_node_in,
    coarse_node_bias,
    coarse_node_out,
):
    nodes = node_features.shape[0]
    features = node_features.T
    (shared,) = call(pick_kernel, [(halo_send.shape[1], WIDTH)], [], halo_send, features)
    rims = exchange(shared)
    updated, payload = call(
        fine_kernel,
        [(WIDTH, nodes), (OWNERS, WIDTH // 2 + 8, 2 * CLUST_DEV)],
        [pltpu.VMEM((WIDTH, 1280), BF16), pltpu.VMEM((WIDTH, nodes), F32)],
        features,
        *rims,
        edge_source,
        edge_target,
        edge_weight_in.T,
        edge_bias[:, None],
        edge_weight_out,
        node_weight_in.T,
        node_bias[:, None],
        node_weight_out,
        cluster_owner.reshape(1, nodes),
        cluster_member.reshape(1, nodes),
    )
    parts = lax.all_to_all(payload, "py", 0, 0, tiled=True)
    coarse, coarse_shared = call(
        coarse_kernel,
        [(WIDTH, CLUST_DEV), (coarse_send.shape[1], WIDTH)],
        [],
        parts,
        coarse_send,
    )
    coarse_rims = exchange(coarse_shared)
    (cluster_updated,) = call(
        level3_kernel,
        [(CLUST_DEV, WIDTH)],
        [],
        coarse,
        *coarse_rims,
        coarse_source,
        coarse_target,
        coarse_edge_in.T,
        coarse_edge_bias[:, None],
        coarse_edge_out,
        coarse_node_in.T,
        coarse_node_bias[:, None],
        coarse_node_out,
    )
    return updated.T, cluster_updated


def solution(mesh):
    split, whole = P(("px", "py"), None), P()
    return jax.shard_map(
        body,
        mesh=mesh,
        in_specs=(split,) * 4
        + (whole,) * 6
        + (split, P(("px", "py")))
        + (split,) * 3
        + (whole,) * 6,
        out_specs=(split, split),
        check_vma=False,
    )
```

time: 141 us -> 73.6 us (0.52)
  the two profiles are of different devices: /device:TPU:31 before, /device:TPU:1 now
where the time goes in v1:
time: 73.6 us; the launch traced here: 73.1 us
  starting transfers between devices  25.4 us (35%)
  blocking collectives  23.5 us (32%)
  Pallas kernels  17 us (23%)
  local copies, waits for them, and re-layouts  5.6 us (8%)
  waiting for transfers between devices  0.86 us (1%)
  between operations  0.76 us (1%)
    all_to_all x1, blocking collectives, body(): parts = lax.all_to_all(payload, 'py', 0, 0, tiled=True)  23.5 us
    pallas_call x4, Pallas kernels, call(): pl.pallas_call(kernel, out_shape=[jax.ShapeDtypeStruct(shape, BF16) for s...  17 us
    ppermute x4, starting transfers between devices, exchange(): found.append(lax.ppermute(shared, axis, [(b, a) for a, b in ahead]))  16.3 us
    ppermute x4, starting transfers between devices, exchange(): found.append(lax.ppermute(shared, axis, ahead))  9.06 us
    unnamed x24, local copies, waits for them, and re-layouts  2.55 us
  transfers between devices with their start and end apart: 8, of which 1 were waited for; matrix products, arithmetic and copies ran while one was open for 4% of the time, Pallas kernels for 0%

profile of v1, /device:TPU:1, one launch (start us, length us, event | category | flops | bytes accessed | tf_op | source)
XLA Modules:
  0.0 73.1 jit_solution(14404190171270487489)
XLA Ops:
  0.6 1.8 %pick_kernel.1 = bf16[64,192]{1,0:T(8,128)(2,1)} custom-call(s32[1,64]{1,0:T(1,128)} %send_ref.2, bf16[192,512]{1,0:T(8,128)(2,1)} %bitcast.12), custom_call_target="tpu_custom_call" | custom-call | tf_op jit(solution)/shard_map/pick_kernel/pallas_call | solution.py:213
  2.4 0.0 copy-start.8
  2.4 4.1 %collective-permute-start = (bf16[64,192]{1,0:T(8,128)(2,1)}, bf16[64,192]{1,0:T(8,128)(2,1)S(1)}, u32[]{:S(2)}, u32[]{:S(2)}) collective-permute-start(bf16[64,192]{1,0:T(8,128)(2,1)} %pick_kernel.1), channel_id=1, source_target_pairs={{0,16},{16,32},{32,48},{48,64},{64,80},{80,96},{96,112},{112,128},... | collective-permute-start | bytes 73736 | tf_op jit(solution)/shard_map/ppermute | solution.py:207
  6.5 6.1 %collective-permute-start.1 = (bf16[64,192]{1,0:T(8,128)(2,1)}, bf16[64,192]{1,0:T(8,128)(2,1)S(1)}, u32[]{:S(2)}, u32[]{:S(2)}) collective-permute-start(bf16[64,192]{1,0:T(8,128)(2,1)} %pick_kernel.1), channel_id=1, source_target_pairs={{16,0},{32,16},{48,32},{64,48},{80,64},{96,80},{112,96},{128,112},... | collective-permute-start | bytes 73736 | tf_op jit(solution)/shard_map/ppermute | solution.py:208
  12.6 2.9 %collective-permute-start.2 = (bf16[64,192]{1,0:T(8,128)(2,1)}, bf16[64,192]{1,0:T(8,128)(2,1)S(1)}, u32[]{:S(2)}, u32[]{:S(2)}) collective-permute-start(bf16[64,192]{1,0:T(8,128)(2,1)} %pick_kernel.1), channel_id=1, source_target_pairs={{0,1},{1,2},{2,3},{3,4},{4,5},{5,6},{6,7},{7,8},{8,9},{9,10},{10,1... | collective-permute-start | bytes 73736 | tf_op jit(solution)/shard_map/ppermute | solution.py:207
  15.5 3.1 %collective-permute-start.3 = (bf16[64,192]{1,0:T(8,128)(2,1)}, bf16[64,192]{1,0:T(8,128)(2,1)S(1)}, u32[]{:S(2)}, u32[]{:S(2)}) collective-permute-start(bf16[64,192]{1,0:T(8,128)(2,1)} %pick_kernel.1), channel_id=1, source_target_pairs={{1,0},{2,1},{3,2},{4,3},{5,4},{6,5},{7,6},{8,7},{9,8},{10,9},{11,1... | collective-permute-start | bytes 73736 | tf_op jit(solution)/shard_map/ppermute | solution.py:208
  18.6 0.0 copy-done.8
  18.6 0.8 %copy.23.bias_ref = f32[192,1]{1,0:T(8,128)} copy(f32[192,1]{0,1:T(1,128)S(1)} %bitcast.20) | data formatting | bytes 1536 | tf_op jit(solution)/shard_map/broadcast_in_dim | solution.py:257
  19.4 0.0 copy-start.9
  19.4 0.7 copy-done.9
  20.0 0.8 %copy.24.nbias_ref = f32[192,1]{1,0:T(8,128)} copy(f32[192,1]{0,1:T(1,128)S(1)} %bitcast.21) | data formatting | bytes 1536 | tf_op jit(solution)/shard_map/broadcast_in_dim | solution.py:260
  20.8 0.0 collective-permute-done.h0
  20.8 0.0 copy-start
  20.8 0.0 collective-permute-done.1.h1
  20.8 0.0 copy-start.1
  20.8 0.0 collective-permute-done.2.h2
  20.8 0.0 copy-start.2
  20.8 0.0 collective-permute-done.3.h3
  20.8 0.0 copy-start.3
  20.9 0.6 copy-done
  21.4 0.0 copy-done.1
  21.4 0.0 copy-done.2
  21.4 0.0 copy-done.3
  21.5 10.1 %fine_kernel.1 = (bf16[192,512]{1,0:T(8,128)(2,1)}, bf16[16,104,128]{2,1,0:T(8,128)(2,1)}) custom-call(bf16[192,512]{1,0:T(8,128)(2,1)} %bitcast.13, bf16[64,192]{1,0:T(8,128)(2,1)} %copy-done, bf16[64,192]{1,0:T(8,128)(2,1)} %copy-done.1, bf16[64,192]{1,0:T(8,128)(2,1)} %copy-done.2, bf16[64,192]{1,0:T(8,128)(2,1)} %copy-done.3, s32[1,3072]{1,0:T(1,128)} %src_ref.2, ...), custom_call_target="tpu_custom_call" | custom-call | tf_op jit(solution)/shard_map/fine_kernel/pallas_call | solution.py:213
  31.6 23.5 %all_to_all.5.parts_ref = bf16[16,104,128]{2,1,0:T(8,128)(2,1)} all-to-all(bf16[16,104,128]{2,1,0:T(8,128)(2,1)} %get-tuple-element.7), channel_id=1, replica_groups=mesh['px'=32,'py'=16] {'py'}, dimensions={0} | all-to-all | bytes 851968 | tf_op jit(solution)/shard_map/all_to_all | solution.py:265
  55.0 1.9 %coarse_kernel.1 = (bf16[192,64]{1,0:T(8,128)(2,1)}, bf16[16,192]{1,0:T(8,128)(2,1)}) custom-call(bf16[16,104,128]{2,1,0:T(8,128)(2,1)} %all_to_all.5.parts_ref, s32[1,16]{1,0:T(1,128)} %send_ref.3), custom_call_target="tpu_custom_call" | custom-call | tf_op jit(solution)/shard_map/coarse_kernel/pallas_call | solution.py:213
  56.9 0.0 copy-start.10
  56.9 2.0 %collective-permute-start.4 = (bf16[16,192]{1,0:T(8,128)(2,1)}, bf16[16,192]{1,0:T(8,128)(2,1)S(1)}, u32[]{:S(2)}, u32[]{:S(2)}) collective-permute-start(bf16[16,192]{1,0:T(8,128)(2,1)} %get-tuple-element.9), channel_id=1, source_target_pairs={{0,16},{16,32},{32,48},{48,64},{64,80},{80,96},{96,112},{112,128},... | collective-permute-start | bytes 18440 | tf_op jit(solution)/shard_map/ppermute | solution.py:207
  59.0 6.7 %collective-permute-start.5 = (bf16[16,192]{1,0:T(8,128)(2,1)}, bf16[16,192]{1,0:T(8,128)(2,1)S(1)}, u32[]{:S(2)}, u32[]{:S(2)}) collective-permute-start(bf16[16,192]{1,0:T(8,128)(2,1)} %get-tuple-element.9), channel_id=1, source_target_pairs={{16,0},{32,16},{48,32},{64,48},{80,64},{96,80},{112,96},{128,112},... | collective-permute-start | bytes 18440 | tf_op jit(solution)/shard_map/ppermute | solution.py:208
  65.7 0.0 collective-permute-start.6
  65.7 0.5 collective-permute-start.7
  66.2 0.0 copy-done.10
  66.2 0.8 %copy.25.bias_ref = f32[192,1]{1,0:T(8,128)} copy(f32[192,1]{0,1:T(1,128)S(1)} %bitcast.22) | data formatting | bytes 1536 | tf_op jit(solution)/shard_map/broadcast_in_dim | solution.py:283
  67.0 0.0 copy-start.11
  67.0 0.7 copy-done.11
  67.6 0.8 %copy.26.nbias_ref = f32[192,1]{1,0:T(8,128)} copy(f32[192,1]{0,1:T(1,128)S(1)} %bitcast.23) | data formatting | bytes 1536 | tf_op jit(solution)/shard_map/broadcast_in_dim | solution.py:286
  68.4 0.0 collective-permute-done.4.h0
  68.4 0.0 copy-start.4
  68.4 0.0 collective-permute-done.5.h1
  68.4 0.0 copy-start.5
  68.4 0.0 collective-permute-done.6.h2
  68.4 0.0 copy-start.6
  68.4 0.8 %collective-permute-done.7.h3 = bf16[16,192]{1,0:T(8,128)(2,1)S(1)} collective-permute-done((bf16[16,192]{1,0:T(8,128)(2,1)}, bf16[16,192]{1,0:T(8,128)(2,1)S(1)}, u32[]{:S(2)}, u32[]{:S(2)}) %collective-permute-start.7) | collective-permute-done | bytes 6176 | tf_op jit(solution)/shard_map/ppermute | solution.py:208
  69.3 0.0 copy-done.4
  69.3 0.0 copy-done.5
  69.3 0.0 copy-done.6
  69.3 0.6 copy-done.7
  69.9 3.3 %level3_kernel.1 = bf16[64,192]{1,0:T(8,128)(2,1)} custom-call(bf16[192,64]{1,0:T(8,128)(2,1)} %get-tuple-element.8.feat_ref, bf16[16,192]{1,0:T(8,128)(2,1)} %copy-done.4, bf16[16,192]{1,0:T(8,128)(2,1)} %copy-done.5, bf16[16,192]{1,0:T(8,128)(2,1)} %copy-done.6, bf16[16,192]{1,0:T(8,128)(2,1)} %copy-done.7, s32[1,384]{1,0:T(1,128)} %src_ref.3, ...), custom_call_target="tpu_custom_call" | custom-call | tf_op jit(solution)/shard_map/level3_kernel/pallas_call | solution.py:213
  (1 shorter events, 0.0 us)
Async XLA Ops:
  2.4 16.2 %copy-start.8 = (f32[192]{0:T(256)S(1)}, f32[192]{0:T(256)}, u32[]{:S(2)}) copy-start(f32[192]{0:T(256)} %param.26) | copy-start | bytes 2308
  2.4 18.4 %collective-permute-start = (bf16[64,192]{1,0:T(8,128)(2,1)}, bf16[64,192]{1,0:T(8,128)(2,1)S(1)}, u32[]{:S(2)}, u32[]{:S(2)}) collective-permute-start(bf16[64,192]{1,0:T(8,128)(2,1)} %pick_kernel.1), channel_id=1, source_target_pairs={{0,16},{16,32},{32,48},{48,64},{64,80},{80,96},{96,112},{112,128},... | collective-permute-start | bytes 73736 | tf_op jit(solution)/shard_map/ppermute | solution.py:207
  6.5 14.3 %collective-permute-start.1 = (bf16[64,192]{1,0:T(8,128)(2,1)}, bf16[64,192]{1,0:T(8,128)(2,1)S(1)}, u32[]{:S(2)}, u32[]{:S(2)}) collective-permute-start(bf16[64,192]{1,0:T(8,128)(2,1)} %pick_kernel.1), channel_id=1, source_target_pairs={{16,0},{32,16},{48,32},{64,48},{80,64},{96,80},{112,96},{128,112},... | collective-permute-start | bytes 73736 | tf_op jit(solution)/shard_map/ppermute | solution.py:208
  12.6 8.2 %collective-permute-start.2 = (bf16[64,192]{1,0:T(8,128)(2,1)}, bf16[64,192]{1,0:T(8,128)(2,1)S(1)}, u32[]{:S(2)}, u32[]{:S(2)}) collective-permute-start(bf16[64,192]{1,0:T(8,128)(2,1)} %pick_kernel.1), channel_id=1, source_target_pairs={{0,1},{1,2},{2,3},{3,4},{4,5},{5,6},{6,7},{7,8},{8,9},{9,10},{10,1... | collective-permute-start | bytes 73736 | tf_op jit(solution)/shard_map/ppermute | solution.py:207
  15.5 5.3 %collective-permute-start.3 = (bf16[64,192]{1,0:T(8,128)(2,1)}, bf16[64,192]{1,0:T(8,128)(2,1)S(1)}, u32[]{:S(2)}, u32[]{:S(2)}) collective-permute-start(bf16[64,192]{1,0:T(8,128)(2,1)} %pick_kernel.1), channel_id=1, source_target_pairs={{1,0},{2,1},{3,2},{4,3},{5,4},{6,5},{7,6},{8,7},{9,8},{10,9},{11,1... | collective-permute-start | bytes 73736 | tf_op jit(solution)/shard_map/ppermute | solution.py:208
  19.4 0.7 copy-start.9
  20.8 0.6 copy-start
  20.8 0.6 copy-start.1
  20.8 0.6 copy-start.2
  20.8 0.6 copy-start.3
  56.9 9.3 %copy-start.10 = (f32[192]{0:T(256)S(1)}, f32[192]{0:T(256)}, u32[]{:S(2)}) copy-start(f32[192]{0:T(256)} %param.37) | copy-start | bytes 2308
  56.9 11.5 %collective-permute-start.4 = (bf16[16,192]{1,0:T(8,128)(2,1)}, bf16[16,192]{1,0:T(8,128)(2,1)S(1)}, u32[]{:S(2)}, u32[]{:S(2)}) collective-permute-start(bf16[16,192]{1,0:T(8,128)(2,1)} %get-tuple-element.9), channel_id=1, source_target_pairs={{0,16},{16,32},{32,48},{48,64},{64,80},{80,96},{96,112},{112,128},... | collective-permute-start | bytes 18440 | tf_op jit(solution)/shard_map/ppermute | solution.py:207
  59.0 9.4 %collective-permute-start.5 = (bf16[16,192]{1,0:T(8,128)(2,1)}, bf16[16,192]{1,0:T(8,128)(2,1)S(1)}, u32[]{:S(2)}, u32[]{:S(2)}) collective-permute-start(bf16[16,192]{1,0:T(8,128)(2,1)} %get-tuple-element.9), channel_id=1, source_target_pairs={{16,0},{32,16},{48,32},{64,48},{80,64},{96,80},{112,96},{128,112},... | collective-permute-start | bytes 18440 | tf_op jit(solution)/shard_map/ppermute | solution.py:208
  65.7 2.8 %collective-permute-start.6 = (bf16[16,192]{1,0:T(8,128)(2,1)}, bf16[16,192]{1,0:T(8,128)(2,1)S(1)}, u32[]{:S(2)}, u32[]{:S(2)}) collective-permute-start(bf16[16,192]{1,0:T(8,128)(2,1)} %get-tuple-element.9), channel_id=1, source_target_pairs={{0,1},{1,2},{2,3},{3,4},{4,5},{5,6},{6,7},{7,8},{8,9},{9,10},{10,1... | collective-permute-start | bytes 18440 | tf_op jit(solution)/shard_map/ppermute | solution.py:207
  65.7 3.6 %collective-permute-start.7 = (bf16[16,192]{1,0:T(8,128)(2,1)}, bf16[16,192]{1,0:T(8,128)(2,1)S(1)}, u32[]{:S(2)}, u32[]{:S(2)}) collective-permute-start(bf16[16,192]{1,0:T(8,128)(2,1)} %get-tuple-element.9), channel_id=1, source_target_pairs={{1,0},{2,1},{3,2},{4,3},{5,4},{6,5},{7,6},{8,7},{9,8},{10,9},{11,1... | collective-permute-start | bytes 18440 | tf_op jit(solution)/shard_map/ppermute | solution.py:208
  67.0 0.7 copy-start.11
  68.4 0.9 %copy-start.4 = (bf16[16,192]{1,0:T(8,128)(2,1)}, bf16[16,192]{1,0:T(8,128)(2,1)S(1)}, u32[]{:S(2)}) copy-start(bf16[16,192]{1,0:T(8,128)(2,1)S(1)} %collective-permute-done.4.h0) | copy-start | bytes 18436
  68.4 0.9 %copy-start.5 = (bf16[16,192]{1,0:T(8,128)(2,1)}, bf16[16,192]{1,0:T(8,128)(2,1)S(1)}, u32[]{:S(2)}) copy-start(bf16[16,192]{1,0:T(8,128)(2,1)S(1)} %collective-permute-done.5.h1) | copy-start | bytes 18436
  68.4 0.9 %copy-start.6 = (bf16[16,192]{1,0:T(8,128)(2,1)}, bf16[16,192]{1,0:T(8,128)(2,1)S(1)}, u32[]{:S(2)}) copy-start(bf16[16,192]{1,0:T(8,128)(2,1)S(1)} %collective-permute-done.6.h2) | copy-start | bytes 18436
  69.3 0.6 copy-start.7

commit v2 on v1

v2 whole, which is shorter than its diff:
```python
import jax
import jax.numpy as jnp
from jax import lax
from jax.experimental import pallas as pl
from jax.experimental.pallas import tpu as pltpu
from jax.sharding import PartitionSpec as P

WIDTH = 192
CLUST_DEV = 64
OWNERS = 16
BLOCK = 1024
F32, BF16, I32, I16 = jnp.float32, jnp.bfloat16, jnp.int32, jnp.int16


def nn(a, b):
    return jnp.dot(a, b, preferred_element_type=F32)


def nt(a, b):
    return lax.dot_general(a, b, (((1,), (1,)), ((), ())), preferred_element_type=F32)


def one_hot_rows(ids, count):
    row = lax.broadcasted_iota(I32, (count, ids.shape[1]), 0).astype(I16)
    return jnp.where(row == ids.astype(I16), jnp.ones_like(row, BF16), jnp.zeros_like(row, BF16))


def one_hot_lanes(ids, count):
    shape = (ids.shape[0], count)
    lane = lax.broadcasted_iota(I32, shape, 1).astype(I16)
    wide = jnp.broadcast_to(ids, (ids.shape[0], 128)).astype(I16)
    found = lane == jnp.tile(wide, (1, count // 128))
    return jnp.where(found, jnp.ones_like(lane, BF16), jnp.zeros_like(lane, BF16))


def half_silu(half):
    return half * jnp.tanh(half) + half


def normed(values, axis):
    center = values - jnp.mean(values, axis=axis, keepdims=True)
    return center * lax.rsqrt(jnp.mean(center * center, axis=axis, keepdims=True) + 1e-05)


def column(row, count):
    shape = (count, count)
    at = lax.broadcasted_iota(I32, shape, 0) == lax.broadcasted_iota(I32, shape, 1)
    return jnp.sum(jnp.where(at, row, 0.0), axis=1, keepdims=True)


def chooser(send, total):
    count = send.shape[1]
    ids = column(send.astype(F32), count).astype(I32)
    lane = lax.broadcasted_iota(I32, (count, total), 1)
    return jnp.where(lane == ids, 1.0, 0.0).astype(BF16)


def inside_flags():
    i, j = lax.axis_index("px"), lax.axis_index("py")
    return (i > 0, i < lax.axis_size("px") - 1, j > 0, j < lax.axis_size("py") - 1)


def halo_rows(refs):
    rows = []
    for ref, inside in zip(refs, inside_flags()):
        rows.append(jnp.where(inside, ref[...].astype(F32), 0.0).astype(BF16))
    return jnp.concatenate(rows, axis=0)


def pick_kernel(send_ref, table_ref, out_ref):
    out_ref[...] = nt(chooser(send_ref[...], table_ref.shape[1]), table_ref[...]).astype(BF16)


def prepare_kernel(
    send3_ref,
    bias_ref,
    nbias_ref,
    wout_ref,
    nout_ref,
    feat_ref,
    win_ref,
    own_ref,
    into_ref,
    cols_ref,
    wide_ref,
    chosen_ref,
):
    chosen_ref[...] = chooser(send3_ref[...], CLUST_DEV)
    features = feat_ref[...]
    own_ref[...] = (0.5 * nn(win_ref[:, :WIDTH], features)).astype(BF16)
    into_ref[...] = (0.5 * nn(win_ref[:, WIDTH:], features)).astype(BF16)
    wide_ref[0] = wout_ref[...].astype(F32).T.astype(BF16)
    wide_ref[1] = nout_ref[...].astype(F32).T.astype(BF16)
    cols_ref[0] = jnp.broadcast_to(column(0.5 * bias_ref[...], WIDTH), (WIDTH, 128))
    cols_ref[1] = jnp.broadcast_to(column(0.5 * nbias_ref[...], WIDTH), (WIDTH, 128))


def fine_kernel(
    feat_ref,
    own_ref,
    into_ref,
    cols_ref,
    wide_ref,
    h0,
    h1,
    h2,
    h3,
    src_ref,
    tgt_ref,
    win_ref,
    nin_ref,
    owner_ref,
    member_ref,
    updated_ref,
    payload_ref,
    picks_ref,
    totals_ref,
):
    nodes = feat_ref.shape[1]
    rim = halo_rows((h0, h1, h2, h3))
    lookups = nodes + rim.shape[0]
    picks_ref[:, :nodes] = own_ref[...]
    picks_ref[:, nodes:lookups] = (0.5 * nt(win_ref[:, :WIDTH], rim)).astype(BF16)
    picks_ref[:, lookups:] = into_ref[...]
    for step in range(src_ref.shape[1] // BLOCK):
        at = pl.ds(step * BLOCK, BLOCK)
        from_source = one_hot_rows(src_ref[:, at], lookups)
        to_target = one_hot_rows(tgt_ref[:, at], nodes)
        half = nn(picks_ref[...], jnp.concatenate([from_source, to_target], axis=0))
        hidden = half_silu(half + jnp.tile(cols_ref[0], (1, BLOCK // 128))).astype(BF16)
        message = normed(nn(wide_ref[0], hidden), 0).astype(BF16)
        added = nt(message, to_target)
        if step == 0:
            totals_ref[...] = added
        else:
            totals_ref[...] += added

    features = feat_ref[...]
    joined = jnp.concatenate([features, totals_ref[...].astype(BF16)], axis=0)
    half = 0.5 * nn(nin_ref[...], joined) + jnp.tile(cols_ref[1], (1, nodes // 128))
    updated = features.astype(F32) + normed(nn(wide_ref[1], half_silu(half).astype(BF16)), 0)
    updated = updated.astype(BF16)
    updated_ref[...] = updated

    position = owner_ref[...] * CLUST_DEV + member_ref[...]
    counted = jnp.concatenate([updated, jnp.ones((16, nodes), BF16)], axis=0)
    member_of = one_hot_rows(position, OWNERS * CLUST_DEV)
    pooled = nt(counted, member_of)
    for pair in range(OWNERS // 2):
        part = pooled[:, pair * 2 * CLUST_DEV : (pair + 1) * 2 * CLUST_DEV]
        half = WIDTH // 2
        top, low, count = part[:half], part[half:WIDTH], part[WIDTH : WIDTH + 8]
        left = lax.broadcasted_iota(I32, (half, 2 * CLUST_DEV), 1) < CLUST_DEV
        payload_ref[2 * pair, :half, :] = jnp.where(
            left, top, pltpu.roll(low, CLUST_DEV, 1)
        ).astype(BF16)
        payload_ref[2 * pair, half:, :] = count.astype(BF16)
        payload_ref[2 * pair + 1, :half, :] = jnp.where(
            left, pltpu.roll(top, CLUST_DEV, 1), low
        ).astype(BF16)
        payload_ref[2 * pair + 1, half:, :] = pltpu.roll(count, CLUST_DEV, 1).astype(BF16)


def coarse_kernel(parts_ref, chosen_ref, coarse_ref, shared_ref):
    total = jnp.sum(parts_ref[...].astype(F32), axis=0)
    half = WIDTH // 2
    sums = jnp.concatenate([total[:half], pltpu.roll(total[:half], CLUST_DEV, 1)], axis=0)
    counts = total[half : half + 1]
    coarse = (sums / jnp.maximum(counts, 1.0)).astype(BF16)[:, :CLUST_DEV]
    coarse_ref[...] = coarse
    shared_ref[...] = nt(chosen_ref[...], coarse).astype(BF16)


def prepare3_kernel(
    src_ref,
    tgt_ref,
    bias_ref,
    nbias_ref,
    wout_ref,
    nout_ref,
    feat_ref,
    win_ref,
    half_ref,
    around_ref,
    target_ref,
    cols_ref,
    wide_ref,
):
    features = feat_ref[...]
    nodes = features.shape[1]
    own = (0.5 * nn(win_ref[:, :WIDTH], features)).astype(BF16)
    into = (0.5 * nn(win_ref[:, WIDTH:], features)).astype(BF16)
    from_own = one_hot_rows(src_ref[...], nodes)
    to_target = one_hot_rows(tgt_ref[...], nodes)
    target_ref[...] = to_target
    around_ref[...] = one_hot_rows(src_ref[...] - nodes, around_ref.shape[0])
    half_ref[...] = nn(own, from_own) + nn(into, to_target) + column(0.5 * bias_ref[...], WIDTH)
    wide_ref[0] = wout_ref[...].astype(F32).T.astype(BF16)
    wide_ref[1] = nout_ref[...].astype(F32).T.astype(BF16)
    cols_ref[...] = jnp.broadcast_to(column(0.5 * nbias_ref[...], WIDTH), (WIDTH, nodes))


def level3_kernel(
    feat_ref,
    half_ref,
    around_ref,
    target_ref,
    cols_ref,
    wide_ref,
    h0,
    h1,
    h2,
    h3,
    win_ref,
    nin_ref,
    updated_ref,
):
    features = feat_ref[...]
    nodes = features.shape[1]
    rim = halo_rows((h0, h1, h2, h3))
    near = (0.5 * nt(win_ref[:, :WIDTH], rim)).astype(BF16)
    hidden = half_silu(half_ref[...] + nn(near, around_ref[...])).astype(BF16)
    message = normed(nn(wide_ref[0], hidden), 0).astype(BF16)
    totals = nt(message, target_ref[...])
    joined = jnp.concatenate([features, totals.astype(BF16)], axis=0)
    hidden = half_silu(0.5 * nn(nin_ref[...], joined) + cols_ref[...]).astype(BF16)
    updated = features.astype(F32) + normed(nn(wide_ref[1], hidden), 0)
    wide = jnp.concatenate([updated, jnp.zeros_like(updated)], axis=1)
    updated_ref[...] = wide.T[:nodes].astype(BF16)


def exchange(shared):
    found = []
    for axis in ("px", "py"):
        count = lax.axis_size(axis)
        ahead = [(k, (k + 1) % count) for k in range(count)]
        found.append(lax.ppermute(shared, axis, ahead))
        found.append(lax.ppermute(shared, axis, [(b, a) for a, b in ahead]))
    return found


def call(kernel, outs, scratch, *args, loose=()):
    held = pl.BlockSpec(memory_space=pltpu.VMEM)
    return pl.pallas_call(
        kernel,
        out_shape=[space(shape, kind) for space, shape, kind in outs],
        in_specs=[held] * (len(loose) + len(args)),
        out_specs=[held] * len(outs),
        scratch_shapes=scratch,
        name=kernel.__name__,
    )(*loose, *[pltpu.with_memory_space_constraint(arg, pltpu.VMEM) for arg in args])


def body(
    node_features,
    edge_source,
    edge_target,
    halo_send,
    edge_weight_in,
    edge_bias,
    edge_weight_out,
    node_weight_in,
    node_bias,
    node_weight_out,
    cluster_owner,
    cluster_member,
    coarse_send,
    coarse_source,
    coarse_target,
    coarse_edge_in,
    coarse_edge_bias,
    coarse_edge_out,
    coarse_node_in,
    coarse_node_bias,
    coarse_node_out,
):
    nodes = node_features.shape[0]
    features = node_features.T
    (shared,) = call(
        pick_kernel,
        [(pltpu.VMEM, (halo_send.shape[1], WIDTH), BF16)],
        [],
        loose=(halo_send, features),
    )
    rims = exchange(shared)
    own, into, cols, wide, chosen = call(
        prepare_kernel,
        [(pltpu.VMEM, (WIDTH, nodes), BF16)] * 2
        + [
            (pltpu.VMEM, (2, WIDTH, 128), F32),
            (pltpu.VMEM, (2, WIDTH, WIDTH), BF16),
            (pltpu.VMEM, (coarse_send.shape[1], CLUST_DEV), BF16),
        ],
        [],
        features,
        edge_weight_in.T,
        loose=(coarse_send, edge_bias[None], node_bias[None], edge_weight_out, node_weight_out),
    )
    updated, payload = call(
        fine_kernel,
        [
            (jax.ShapeDtypeStruct, (WIDTH, nodes), BF16),
            (pltpu.VMEM, (OWNERS, WIDTH // 2 + 8, 2 * CLUST_DEV), BF16),
        ],
        [pltpu.VMEM((WIDTH, 1280), BF16), pltpu.VMEM((WIDTH, nodes), F32)],
        features,
        own,
        into,
        cols,
        wide,
        *rims,
        edge_source,
        edge_target,
        edge_weight_in.T,
        node_weight_in.T,
        cluster_owner.reshape(1, nodes),
        cluster_member.reshape(1, nodes),
    )
    parts = lax.all_to_all(payload, "py", 0, 0, tiled=True)
    coarse, coarse_shared = call(
        coarse_kernel,
        [
            (pltpu.VMEM, (WIDTH, CLUST_DEV), BF16),
            (pltpu.VMEM, (coarse_send.shape[1], WIDTH), BF16),
        ],
        [],
        parts,
        chosen,
    )
    coarse_rims = exchange(coarse_shared)
    links = coarse_source.shape[1]
    prepared = call(
        prepare3_kernel,
        [
            (pltpu.VMEM, (WIDTH, links), F32),
            (pltpu.VMEM, (4 * coarse_send.shape[1], links), BF16),
            (pltpu.VMEM, (CLUST_DEV, links), BF16),
            (pltpu.VMEM, (WIDTH, CLUST_DEV), F32),
            (pltpu.VMEM, (2, WIDTH, WIDTH), BF16),
        ],
        [],
        coarse,
        coarse_edge_in.T,
        loose=(
            coarse_source,
            coarse_target,
            coarse_edge_bias[None],
            coarse_node_bias[None],
            coarse_edge_out,
            coarse_node_out,
        ),
    )
    (cluster_updated,) = call(
        level3_kernel,
        [(jax.ShapeDtypeStruct, (CLUST_DEV, WIDTH), BF16)],
        [],
        coarse,
        *prepared,
        *coarse_rims,
        coarse_edge_in.T,
        coarse_node_in.T,
    )
    return updated.T, cluster_updated


def solution(mesh):
    split, whole = P(("px", "py"), None), P()
    return jax.shard_map(
        body,
        mesh=mesh,
        in_specs=(split,) * 4
        + (whole,) * 6
        + (split, P(("px", "py")))
        + (split,) * 3
        + (whole,) * 6,
        out_specs=(split, split),
        check_vma=False,
    )
```

time: 73.6 us -> 66.6 us (0.905)
  waiting for transfers between devices: 0.86 us -> 8.04 us
  Pallas kernels: 17 us -> 10.8 us
  starting transfers between devices: 25.4 us -> 19.9 us
  local copies, waits for them, and re-layouts: 5.6 us -> 0.94 us
  blocking collectives: 23.5 us -> 25.7 us
    ppermute x4, waiting for transfers between devices: 0.01 us -> 8.03 us  [exchange(): found.append(lax.ppermute(shared, axis, ahead))]
    pallas_call x4 -> x6, Pallas kernels: 17 us -> 10.8 us  [call(): pl.pallas_call(kernel, out_shape=[space(shape, kind) for space, shape, ki...]
    ppermute x4, starting transfers between devices: 9.06 us -> 5.6 us  [exchange(): found.append(lax.ppermute(shared, axis, ahead))]
    broadcast_in_dim x4 -> x0, local copies, waits for them, and re-layouts: 3.05 us -> none  [the longest x1 0.77 us: body(): coarse_edge_bias[:, None]]
    all_to_all x1, blocking collectives: 23.5 us -> 25.7 us  [body(): parts = lax.all_to_all(payload, 'py', 0, 0, tiled=True)]
    ppermute x4, starting transfers between devices: 16.3 us -> 14.3 us  [exchange(): found.append(lax.ppermute(shared, axis, [(b, a) for a, b in ahead]))]
    unnamed x24 -> x18, local copies, waits for them, and re-layouts: 2.55 us -> 0.94 us
    ppermute x4, waiting for transfers between devices: 0.85 us -> 0.01 us  [exchange(): found.append(lax.ppermute(shared, axis, [(b, a) for a, b in ahead]))]
  transfers between devices with their start and end apart: 8 -> 8, of which waited for: 1 -> 2; matrix products, arithmetic and copies ran while one was open for 4% -> 0% of each run, Pallas kernels for 0% -> 4%
where the time goes in v2:
time: 66.6 us; the launch traced here: 66.2 us
  blocking collectives  25.7 us (39%)
  starting transfers between devices  19.9 us (30%)
  Pallas kernels  10.8 us (16%)
  waiting for transfers between devices  8.04 us (12%)
  local copies, waits for them, and re-layouts  0.94 us (1%)
  between operations  0.8 us (1%)
    all_to_all x1, blocking collectives, body(): parts = lax.all_to_all(payload, 'py', 0, 0, tiled=True)  25.7 us
    ppermute x4, starting transfers between devices, exchange(): found.append(lax.ppermute(shared, axis, [(b, a) for a, b in ahead]))  14.3 us
    pallas_call x6, Pallas kernels, call(): pl.pallas_call(kernel, out_shape=[space(shape, kind) for space, shape, ki...  10.8 us
    ppermute x4, waiting for transfers between devices, exchange(): found.append(lax.ppermute(shared, axis, ahead))  8.03 us
    ppermute x4, starting transfers between devices, exchange(): found.append(lax.ppermute(shared, axis, ahead))  5.6 us
  transfers between devices with their start and end apart: 8, of which 2 were waited for; matrix products, arithmetic and copies ran while one was open for 0% of the time, Pallas kernels for 4%

profile of v2, /device:TPU:1, one launch (start us, length us, event | category | flops | bytes accessed | tf_op | source)
XLA Modules:
  0.0 66.2 jit_solution(10753535639343589994)
XLA Ops:
  0.6 0.0 copy-start
  0.6 1.2 %pick_kernel.1 = bf16[64,192]{1,0:T(8,128)(2,1)S(1)} custom-call(s32[1,64]{1,0:T(1,128)} %send_ref.1, bf16[192,512]{1,0:T(8,128)(2,1)} %bitcast.12), custom_call_target="tpu_custom_call" | custom-call | tf_op jit(solution)/shard_map/pick_kernel/pallas_call | solution.py:244
  1.9 6.8 %collective-permute-start.3 = (bf16[64,192]{1,0:T(8,128)(2,1)S(1)}, bf16[64,192]{1,0:T(8,128)(2,1)S(1)}, u32[]{:S(2)}, u32[]{:S(2)}) collective-permute-start(bf16[64,192]{1,0:T(8,128)(2,1)S(1)} %pick_kernel.1), channel_id=1, source_target_pairs={{1,0},{2,1},{3,2},{4,3},{5,4},{6,5},{7,6},{8,7},{9,8},{10,9},{11,1... | collective-permute-start | bytes 73736 | tf_op jit(solution)/shard_map/ppermute | solution.py:238
  8.7 0.0 collective-permute-start.2
  8.7 3.9 %collective-permute-start.1 = (bf16[64,192]{1,0:T(8,128)(2,1)S(1)}, bf16[64,192]{1,0:T(8,128)(2,1)S(1)}, u32[]{:S(2)}, u32[]{:S(2)}) collective-permute-start(bf16[64,192]{1,0:T(8,128)(2,1)S(1)} %pick_kernel.1), channel_id=1, source_target_pairs={{16,0},{32,16},{48,32},{64,48},{80,64},{96,80},{112,96},{128,112},... | collective-permute-start | bytes 73736 | tf_op jit(solution)/shard_map/ppermute | solution.py:238
  12.6 1.9 %collective-permute-start = (bf16[64,192]{1,0:T(8,128)(2,1)S(1)}, bf16[64,192]{1,0:T(8,128)(2,1)S(1)}, u32[]{:S(2)}, u32[]{:S(2)}) collective-permute-start(bf16[64,192]{1,0:T(8,128)(2,1)S(1)} %pick_kernel.1), channel_id=1, source_target_pairs={{0,16},{16,32},{32,48},{48,64},{64,80},{80,96},{96,112},{112,128},... | collective-permute-start | bytes 73736 | tf_op jit(solution)/shard_map/ppermute | solution.py:237
  14.6 0.0 copy-done
  14.6 0.0 copy-start.2
  14.6 0.9 %copy-done.2 = bf16[384,192]{0,1:T(8,128)(2,1)S(1)} copy-done((bf16[384,192]{0,1:T(8,128)(2,1)S(1)}, bf16[384,192]{0,1:T(8,128)(2,1)}, u32[]{:S(2)}) %copy-start.2) | copy-done | bytes 147480
  15.5 0.0 copy-start.4
  15.5 0.0 copy-start.6
  15.5 0.0 copy-start.7
  15.5 0.0 copy-start.8
  15.5 1.3 %prepare_kernel.1 = (bf16[192,512]{1,0:T(8,128)(2,1)S(1)}, bf16[192,512]{1,0:T(8,128)(2,1)S(1)}, f32[2,192,128]{2,1,0:T(8,128)S(1)}, bf16[2,192,192]{2,1,0:T(8,128)(2,1)S(1)}, bf16[16,64]{1,0:T(8,128)(2,1)S(1)}) custom-call(s32[1,16]{1,0:T(1,128)} %send3_ref.1, f32[1,192]{1,0:T(1,128)} %bitcast.23, f32[1,192]{1,0:T(1,128)} %bitcast.24, ...), custom_call_target="tpu_custom_call" | custom-call | tf_op jit(solution)/shard_map/prepare_kernel/pallas_call | solution.py:244
  16.8 0.0 copy-start.5
  16.8 0.0 collective-permute-done.3.h3
  16.8 0.0 collective-permute-done.2.h2
  16.9 0.0 collective-permute-done.1.h1
  16.9 3.8 %collective-permute-done.h0 = bf16[64,192]{1,0:T(8,128)(2,1)S(1)} collective-permute-done((bf16[64,192]{1,0:T(8,128)(2,1)S(1)}, bf16[64,192]{1,0:T(8,128)(2,1)S(1)}, u32[]{:S(2)}, u32[]{:S(2)}) %collective-permute-start) | collective-permute-done | bytes 24608 | tf_op jit(solution)/shard_map/ppermute | solution.py:237
  20.6 0.0 copy-done.4
  20.6 0.0 copy-done.6
  20.6 0.0 copy-done.7
  20.6 0.0 copy-done.8
  20.6 0.0 copy-done.5
  20.7 4.8 %fine_kernel.1 = (bf16[192,512]{1,0:T(8,128)(2,1)}, bf16[16,104,128]{2,1,0:T(8,128)(2,1)S(1)}) custom-call(bf16[192,512]{1,0:T(8,128)(2,1)S(1)} %bitcast.14, bf16[192,512]{1,0:T(8,128)(2,1)S(1)} %get-tuple-element.16.own_ref, bf16[192,512]{1,0:T(8,128)(2,1)S(1)} %get-tuple-element.17.into_ref, f32[2,192,128]{2,1,0:T(8,128)S(1)} %get-tuple-element.18.cols_ref, ...), custom_call_target="tpu_custom_call" | custom-call | tf_op jit(solution)/shard_map/fine_kernel/pallas_call | solution.py:244
  25.4 25.7 %all_to_all.5.parts_ref = bf16[16,104,128]{2,1,0:T(8,128)(2,1)S(1)} all-to-all(bf16[16,104,128]{2,1,0:T(8,128)(2,1)S(1)} %get-tuple-element.21), channel_id=1, replica_groups=mesh['px'=32,'py'=16] {'py'}, dimensions={0} | all-to-all | bytes 851968 | tf_op jit(solution)/shard_map/all_to_all | solution.py:319
  51.1 0.0 copy-start.1
  51.1 0.2 coarse_kernel.1
  51.4 0.0 collective-permute-start.7
  51.4 1.8 %collective-permute-start.6 = (bf16[16,192]{1,0:T(8,128)(2,1)S(1)}, bf16[16,192]{1,0:T(8,128)(2,1)S(1)}, u32[]{:S(2)}, u32[]{:S(2)}) collective-permute-start(bf16[16,192]{1,0:T(8,128)(2,1)S(1)} %get-tuple-element.29), channel_id=1, source_target_pairs={{0,1},{1,2},{2,3},{3,4},{4,5},{5,6},{6,7},{7,8},{8,9},{9,10},{10,1... | collective-permute-start | bytes 18440 | tf_op jit(solution)/shard_map/ppermute | solution.py:237
  53.1 3.6 %collective-permute-start.5 = (bf16[16,192]{1,0:T(8,128)(2,1)S(1)}, bf16[16,192]{1,0:T(8,128)(2,1)S(1)}, u32[]{:S(2)}, u32[]{:S(2)}) collective-permute-start(bf16[16,192]{1,0:T(8,128)(2,1)S(1)} %get-tuple-element.29), channel_id=1, source_target_pairs={{16,0},{32,16},{48,32},{64,48},{80,64},{96,80},{112,96},{128,112},... | collective-permute-start | bytes 18440 | tf_op jit(solution)/shard_map/ppermute | solution.py:238
  56.7 1.9 %collective-permute-start.4 = (bf16[16,192]{1,0:T(8,128)(2,1)S(1)}, bf16[16,192]{1,0:T(8,128)(2,1)S(1)}, u32[]{:S(2)}, u32[]{:S(2)}) collective-permute-start(bf16[16,192]{1,0:T(8,128)(2,1)S(1)} %get-tuple-element.29), channel_id=1, source_target_pairs={{0,16},{16,32},{32,48},{48,64},{64,80},{80,96},{96,112},{112,128},... | collective-permute-start | bytes 18440 | tf_op jit(solution)/shard_map/ppermute | solution.py:237
  58.6 0.0 copy-done.1
  58.6 0.0 copy-start.3
  58.6 1.5 %prepare3_kernel.1 = (f32[192,384]{1,0:T(8,128)S(1)}, bf16[64,384]{1,0:T(8,128)(2,1)S(1)}, bf16[64,384]{1,0:T(8,128)(2,1)S(1)}, f32[192,64]{1,0:T(8,128)S(1)}, bf16[2,192,192]{2,1,0:T(8,128)(2,1)S(1)}) custom-call(s32[1,384]{1,0:T(1,128)} %src_ref.3, s32[1,384]{1,0:T(1,128)} %tgt_ref.3, f32[1,192]{1,0:T(1,128)} %bitcast.25, f32[1,192]{1,0:T(1,128)} %bitcast.26, ...), custom_call_target="tpu_custom_call" | custom-call | tf_op jit(solution)/shard_map/prepare3_kernel/pallas_call | solution.py:244
  60.1 0.0 collective-permute-done.7.h3
  60.1 0.0 collective-permute-done.6.h2
  60.1 0.0 collective-permute-done.5.h1
  60.1 4.3 %collective-permute-done.4.h0 = bf16[16,192]{1,0:T(8,128)(2,1)S(1)} collective-permute-done((bf16[16,192]{1,0:T(8,128)(2,1)S(1)}, bf16[16,192]{1,0:T(8,128)(2,1)S(1)}, u32[]{:S(2)}, u32[]{:S(2)}) %collective-permute-start.4) | collective-permute-done | bytes 6176 | tf_op jit(solution)/shard_map/ppermute | solution.py:237
  64.4 0.0 copy-done.3
  64.4 1.8 %level3_kernel.1 = bf16[64,192]{1,0:T(8,128)(2,1)} custom-call(bf16[192,64]{1,0:T(8,128)(2,1)S(1)} %get-tuple-element.23.feat_ref, f32[192,384]{1,0:T(8,128)S(1)} %get-tuple-element.24.half_ref, bf16[64,384]{1,0:T(8,128)(2,1)S(1)} %get-tuple-element.25.around_ref, bf16[64,384]{1,0:T(8,128)(2,1)S(1)} %get-tuple-element.26.target_ref, ...), custom_call_target="tpu_custom_call" | custom-call | tf_op jit(solution)/shard_map/level3_kernel/pallas_call | solution.py:244
Async XLA Ops:
  0.6 13.9 %copy-start = (bf16[512,192]{0,1:T(8,128)(2,1)S(1)}, bf16[512,192]{0,1:T(8,128)(2,1)}, u32[]{:S(2)}) copy-start(bf16[512,192]{0,1:T(8,128)(2,1)} %param.21) | copy-start | bytes 589828
  1.9 15.0 %collective-permute-start.3 = (bf16[64,192]{1,0:T(8,128)(2,1)S(1)}, bf16[64,192]{1,0:T(8,128)(2,1)S(1)}, u32[]{:S(2)}, u32[]{:S(2)}) collective-permute-start(bf16[64,192]{1,0:T(8,128)(2,1)S(1)} %pick_kernel.1), channel_id=1, source_target_pairs={{1,0},{2,1},{3,2},{4,3},{5,4},{6,5},{7,6},{8,7},{9,8},{10,9},{11,1... | collective-permute-start | bytes 73736 | tf_op jit(solution)/shard_map/ppermute | solution.py:238
  8.7 8.2 %collective-permute-start.2 = (bf16[64,192]{1,0:T(8,128)(2,1)S(1)}, bf16[64,192]{1,0:T(8,128)(2,1)S(1)}, u32[]{:S(2)}, u32[]{:S(2)}) collective-permute-start(bf16[64,192]{1,0:T(8,128)(2,1)S(1)} %pick_kernel.1), channel_id=1, source_target_pairs={{0,1},{1,2},{2,3},{3,4},{4,5},{5,6},{6,7},{7,8},{8,9},{9,10},{10,1... | collective-permute-start | bytes 73736 | tf_op jit(solution)/shard_map/ppermute | solution.py:237
  8.7 8.2 %collective-permute-start.1 = (bf16[64,192]{1,0:T(8,128)(2,1)S(1)}, bf16[64,192]{1,0:T(8,128)(2,1)S(1)}, u32[]{:S(2)}, u32[]{:S(2)}) collective-permute-start(bf16[64,192]{1,0:T(8,128)(2,1)S(1)} %pick_kernel.1), channel_id=1, source_target_pairs={{16,0},{32,16},{48,32},{64,48},{80,64},{96,80},{112,96},{128,112},... | collective-permute-start | bytes 73736 | tf_op jit(solution)/shard_map/ppermute | solution.py:238
  12.6 8.0 %collective-permute-start = (bf16[64,192]{1,0:T(8,128)(2,1)S(1)}, bf16[64,192]{1,0:T(8,128)(2,1)S(1)}, u32[]{:S(2)}, u32[]{:S(2)}) collective-permute-start(bf16[64,192]{1,0:T(8,128)(2,1)S(1)} %pick_kernel.1), channel_id=1, source_target_pairs={{0,16},{16,32},{32,48},{48,64},{64,80},{80,96},{96,112},{112,128},... | collective-permute-start | bytes 73736 | tf_op jit(solution)/shard_map/ppermute | solution.py:237
  14.6 0.9 %copy-start.2 = (bf16[384,192]{0,1:T(8,128)(2,1)S(1)}, bf16[384,192]{0,1:T(8,128)(2,1)}, u32[]{:S(2)}) copy-start(bf16[384,192]{0,1:T(8,128)(2,1)} %param.25) | copy-start | bytes 442372
  15.5 5.1 %copy-start.4 = (bf16[384,192]{0,1:T(8,128)(2,1)S(1)}, bf16[384,192]{0,1:T(8,128)(2,1)}, u32[]{:S(2)}) copy-start(bf16[384,192]{0,1:T(8,128)(2,1)} %param.28) | copy-start | bytes 442372
  15.5 5.1 %copy-start.6 = (s32[1,3072]{1,0:T(1,128)S(1)}, s32[1,3072]{1,0:T(1,128)}, u32[]{:S(2)}) copy-start(s32[1,3072]{1,0:T(1,128)} %tgt_ref.2) | copy-start | bytes 36868
  15.5 5.1 %copy-start.7 = (s32[512,1]{0,1:T(1,128)S(1)}, s32[512,1]{0,1:T(1,128)}, u32[]{:S(2)}) copy-start(s32[512,1]{0,1:T(1,128)} %param.31) | copy-start | bytes 6148
  15.5 5.1 %copy-start.8 = (s32[512]{0:T(512)S(1)}, s32[512]{0:T(512)}, u32[]{:S(2)}) copy-start(s32[512]{0:T(512)} %param.32) | copy-start | bytes 6148
  16.8 3.8 %copy-start.5 = (s32[1,3072]{1,0:T(1,128)S(1)}, s32[1,3072]{1,0:T(1,128)}, u32[]{:S(2)}) copy-start(s32[1,3072]{1,0:T(1,128)} %src_ref.2) | copy-start | bytes 36868
  51.1 7.5 %copy-start.1 = (bf16[384,192]{0,1:T(8,128)(2,1)S(1)}, bf16[384,192]{0,1:T(8,128)(2,1)}, u32[]{:S(2)}) copy-start(bf16[384,192]{0,1:T(8,128)(2,1)} %param.36) | copy-start | bytes 442372
  51.4 8.7 %collective-permute-start.7 = (bf16[16,192]{1,0:T(8,128)(2,1)S(1)}, bf16[16,192]{1,0:T(8,128)(2,1)S(1)}, u32[]{:S(2)}, u32[]{:S(2)}) collective-permute-start(bf16[16,192]{1,0:T(8,128)(2,1)S(1)} %get-tuple-element.29), channel_id=1, source_target_pairs={{1,0},{2,1},{3,2},{4,3},{5,4},{6,5},{7,6},{8,7},{9,8},{10,9},{11,1... | collective-permute-start | bytes 18440 | tf_op jit(solution)/shard_map/ppermute | solution.py:238
  51.4 8.7 %collective-permute-start.6 = (bf16[16,192]{1,0:T(8,128)(2,1)S(1)}, bf16[16,192]{1,0:T(8,128)(2,1)S(1)}, u32[]{:S(2)}, u32[]{:S(2)}) collective-permute-start(bf16[16,192]{1,0:T(8,128)(2,1)S(1)} %get-tuple-element.29), channel_id=1, source_target_pairs={{0,1},{1,2},{2,3},{3,4},{4,5},{5,6},{6,7},{7,8},{8,9},{9,10},{10,1... | collective-permute-start | bytes 18440 | tf_op jit(solution)/shard_map/ppermute | solution.py:237
  53.1 7.0 %collective-permute-start.5 = (bf16[16,192]{1,0:T(8,128)(2,1)S(1)}, bf16[16,192]{1,0:T(8,128)(2,1)S(1)}, u32[]{:S(2)}, u32[]{:S(2)}) collective-permute-start(bf16[16,192]{1,0:T(8,128)(2,1)S(1)} %get-tuple-element.29), channel_id=1, source_target_pairs={{16,0},{32,16},{48,32},{64,48},{80,64},{96,80},{112,96},{128,112},... | collective-permute-start | bytes 18440 | tf_op jit(solution)/shard_map/ppermute | solution.py:238
  56.7 7.7 %collective-permute-start.4 = (bf16[16,192]{1,0:T(8,128)(2,1)S(1)}, bf16[16,192]{1,0:T(8,128)(2,1)S(1)}, u32[]{:S(2)}, u32[]{:S(2)}) collective-permute-start(bf16[16,192]{1,0:T(8,128)(2,1)S(1)} %get-tuple-element.29), channel_id=1, source_target_pairs={{0,16},{16,32},{32,48},{48,64},{64,80},{80,96},{96,112},{112,128},... | collective-permute-start | bytes 18440 | tf_op jit(solution)/shard_map/ppermute | solution.py:237
  58.6 5.8 %copy-start.3 = (bf16[384,192]{0,1:T(8,128)(2,1)S(1)}, bf16[384,192]{0,1:T(8,128)(2,1)}, u32[]{:S(2)}) copy-start(bf16[384,192]{0,1:T(8,128)(2,1)} %param.39) | copy-start | bytes 442372

commit v3 on v2

--- a/solution.py
+++ b/solution.py
@@ -67,8 +67,17 @@
     return jnp.concatenate(rows, axis=0)
 
 
-def pick_kernel(send_ref, table_ref, out_ref):
-    out_ref[...] = nt(chooser(send_ref[...], table_ref.shape[1]), table_ref[...]).astype(BF16)
+def pick_kernel(*refs):
+    count = (len(refs) - 2) // 2
+    sources, out_ref, targets, sems = refs[:count], refs[count], refs[count + 1 : -1], refs[-1]
+    copies = fetch(sources, targets, sems)
+    copies[0].wait()
+    copies[1].wait()
+    send_ref, table_ref = targets[:2]
+    chosen = chooser(send_ref[...], table_ref.shape[1])
+    out_ref[...] = nt(chosen, table_ref[...]).astype(BF16)
+    for copy in copies[2:]:
+        copy.wait()
 
 
 def prepare_kernel(
@@ -95,7 +104,20 @@
     cols_ref[1] = jnp.broadcast_to(column(0.5 * nbias_ref[...], WIDTH), (WIDTH, 128))
 
 
-def fine_kernel(
+def fine_kernel(*refs):
+    far = (len(refs) - 22) // 2
+    sources, near, refs = refs[:far], refs[far : far + 15], refs[far + 15 :]
+    (updated_ref, payload_ref), targets, refs = refs[:2], refs[2 : 2 + far], refs[2 + far :]
+    picks_ref, totals_ref, result_ref, sems, result_sem = refs
+    copies = fetch(sources, targets, sems)
+    leave = pltpu.make_async_copy(result_ref, updated_ref, result_sem)
+    fine_round(*near, result_ref, leave, payload_ref, picks_ref, totals_ref)
+    for copy in copies:
+        copy.wait()
+    leave.wait()
+
+
+def fine_round(
     feat_ref,
     own_ref,
     into_ref,
@@ -112,6 +134,7 @@
     owner_ref,
     member_ref,
     updated_ref,
+    leave,
     payload_ref,
     picks_ref,
     totals_ref,
@@ -141,6 +164,7 @@
     updated = features.astype(F32) + normed(nn(wide_ref[1], half_silu(half).astype(BF16)), 0)
     updated = updated.astype(BF16)
     updated_ref[...] = updated
+    leave.start()
 
     position = owner_ref[...] * CLUST_DEV + member_ref[...]
     counted = jnp.concatenate([updated, jnp.ones((16, nodes), BF16)], axis=0)
@@ -231,24 +255,36 @@
 
 def exchange(shared):
     found = []
-    for axis in ("px", "py"):
+    for axis, closed in (("px", False), ("py", True)):
         count = lax.axis_size(axis)
-        ahead = [(k, (k + 1) % count) for k in range(count)]
+        ahead = [(k, (k + 1) % count) for k in range(count if closed else count - 1)]
         found.append(lax.ppermute(shared, axis, ahead))
         found.append(lax.ppermute(shared, axis, [(b, a) for a, b in ahead]))
     return found
 
 
-def call(kernel, outs, scratch, *args, loose=()):
-    held = pl.BlockSpec(memory_space=pltpu.VMEM)
+def fetch(sources, targets, sems):
+    copies = [
+        pltpu.make_async_copy(source, target, sems.at[k])
+        for k, (source, target) in enumerate(zip(sources, targets))
+    ]
+    for copy in copies:
+        copy.start()
+    return copies
+
+
+def call(kernel, outs, scratch, *args, far=(), leave=()):
+    held, away = pl.BlockSpec(memory_space=pltpu.VMEM), pl.BlockSpec(memory_space=pl.ANY)
     return pl.pallas_call(
         kernel,
-        out_shape=[space(shape, kind) for space, shape, kind in outs],
-        in_specs=[held] * (len(loose) + len(args)),
-        out_specs=[held] * len(outs),
+        out_shape=[
+            (jax.ShapeDtypeStruct if k in leave else pltpu.VMEM)(*out) for k, out in enumerate(outs)
+        ],
+        in_specs=[away] * len(far) + [held] * len(args),
+        out_specs=[away if far and k in leave else held for k in range(len(outs))],
         scratch_shapes=scratch,
         name=kernel.__name__,
-    )(*loose, *[pltpu.with_memory_space_constraint(arg, pltpu.VMEM) for arg in args])
+    )(*far, *[pltpu.with_memory_space_constraint(arg, pltpu.VMEM) for arg in args])
 
 
 def body(
@@ -275,54 +311,89 @@
     coarse_node_out,
 ):
     nodes = node_features.shape[0]
-    features = node_features.T
-    (shared,) = call(
+    outs = lambda arrays: [(array.shape, array.dtype) for array in arrays]
+    dma = pltpu.SemaphoreType.DMA
+    held = (
+        halo_send,
+        node_features.T,
+        coarse_send,
+        edge_bias[None],
+        node_bias[None],
+        edge_weight_out,
+        node_weight_out,
+        edge_weight_in.T,
+        node_weight_in.T,
+        edge_source,
+        edge_target,
+        cluster_owner.reshape(1, nodes),
+        cluster_member.reshape(1, nodes),
+    )
+    shared, _, features, send3, bias, nbias, w_out, n_out, w_in, n_in, *ids = call(
         pick_kernel,
-        [(pltpu.VMEM, (halo_send.shape[1], WIDTH), BF16)],
-        [],
-        loose=(halo_send, features),
+        [((halo_send.shape[1], WIDTH), BF16)] + outs(held),
+        [dma((len(held),))],
+        far=held,
     )
     rims = exchange(shared)
     own, into, cols, wide, chosen = call(
         prepare_kernel,
-        [(pltpu.VMEM, (WIDTH, nodes), BF16)] * 2
-        + [
-            (pltpu.VMEM, (2, WIDTH, 128), F32),
-            (pltpu.VMEM, (2, WIDTH, WIDTH), BF16),
-            (pltpu.VMEM, (coarse_send.shape[1], CLUST_DEV), BF16),
+        [
+            ((WIDTH, nodes), BF16),
+            ((WIDTH, nodes), BF16),
+            ((2, WIDTH, 128), F32),
+            ((2, WIDTH, WIDTH), BF16),
+            ((coarse_send.shape[1], CLUST_DEV), BF16),
         ],
         [],
+        send3,
+        bias,
+        nbias,
+        w_out,
+        n_out,
         features,
-        edge_weight_in.T,
-        loose=(coarse_send, edge_bias[None], node_bias[None], edge_weight_out, node_weight_out),
-    )
-    updated, payload = call(
+        w_in,
+    )
+    source, target, owner, member = ids
+    far3 = (
+        coarse_source,
+        coarse_target,
+        coarse_edge_bias[None],
+        coarse_node_bias[None],
+        coarse_edge_out,
+        coarse_node_out,
+        coarse_edge_in.T,
+        coarse_node_in.T,
+    )
+    updated, payload, *held3 = call(
         fine_kernel,
+        [((WIDTH, nodes), BF16), ((OWNERS, WIDTH // 2 + 8, 2 * CLUST_DEV), BF16)] + outs(far3),
         [
-            (jax.ShapeDtypeStruct, (WIDTH, nodes), BF16),
-            (pltpu.VMEM, (OWNERS, WIDTH // 2 + 8, 2 * CLUST_DEV), BF16),
+            pltpu.VMEM((WIDTH, 1280), BF16),
+            pltpu.VMEM((WIDTH, nodes), F32),
+            pltpu.VMEM((WIDTH, nodes), BF16),
+            dma((len(far3),)),
+            dma,
         ],
-        [pltpu.VMEM((WIDTH, 1280), BF16), pltpu.VMEM((WIDTH, nodes), F32)],
         features,
         own,
         into,
         cols,
         wide,
         *rims,
-        edge_source,
-        edge_target,
-        edge_weight_in.T,
-        node_weight_in.T,
-        cluster_owner.reshape(1, nodes),
-        cluster_member.reshape(1, nodes),
-    )
+        source,
+        target,
+        w_in,
+        n_in,
+        owner,
+        member,
+        far=far3,
+        leave=(0,),
+    )
+    w_in3, n_in3 = held3[6:]
     parts = lax.all_to_all(payload, "py", 0, 0, tiled=True)
     coarse, coarse_shared = call(
         coarse_kernel,
-        [
-            (pltpu.VMEM, (WIDTH, CLUST_DEV), BF16),
-            (pltpu.VMEM, (coarse_send.shape[1], WIDTH), BF16),
-        ],
+        [((WIDTH, CLUST_DEV), BF16), ((coarse_send.shape[1], WIDTH), BF16)],
         [],
         parts,
         chosen,
@@ -332,33 +403,27 @@
     prepared = call(
         prepare3_kernel,
         [
-            (pltpu.VMEM, (WIDTH, links), F32),
-            (pltpu.VMEM, (4 * coarse_send.shape[1], links), BF16),
-            (pltpu.VMEM, (CLUST_DEV, links), BF16),
-            (pltpu.VMEM, (WIDTH, CLUST_DEV), F32),
-            (pltpu.VMEM, (2, WIDTH, WIDTH), BF16),
+            ((WIDTH, links), F32),
+            ((4 * coarse_send.shape[1], links), BF16),
+            ((CLUST_DEV, links), BF16),
+            ((WIDTH, CLUST_DEV), F32),
+            ((2, WIDTH, WIDTH), BF16),
         ],
         [],
+        *held3[:6],
         coarse,
-        coarse_edge_in.T,
-        loose=(
-            coarse_source,
-            coarse_target,
-            coarse_edge_bias[None],
-            coarse_node_bias[None],
-            coarse_edge_out,
-            coarse_node_out,
-        ),
+        w_in3,
     )
     (cluster_updated,) = call(
         level3_kernel,
-        [(jax.ShapeDtypeStruct, (CLUST_DEV, WIDTH), BF16)],
+        [((CLUST_DEV, WIDTH), BF16)],
         [],
         coarse,
         *prepared,
         *coarse_rims,
-        coarse_edge_in.T,
-        coarse_node_in.T,
+        w_in3,
+        n_in3,
+        leave=(0,),
     )
     return updated.T, cluster_updated
 

time: 66.6 us -> 62.5 us (0.938)
  the two profiles are of different devices: /device:TPU:1 before, /device:TPU:33 now
where the time goes in v3:
time: 62.5 us; the launch traced here: 62.2 us
  blocking collectives  25.7 us (41%)
  starting transfers between devices  15.9 us (25%)
  Pallas kernels  10.2 us (16%)
  waiting for transfers between devices  9.63 us (15%)
  between operations  0.73 us (1%)
    all_to_all x1, blocking collectives, body(): parts = lax.all_to_all(payload, 'py', 0, 0, tiled=True)  25.7 us
    pallas_call x6, Pallas kernels, call(): pl.pallas_call(kernel, out_shape=[(jax.ShapeDtypeStruct if k in leave els...  10.2 us
    ppermute x4, waiting for transfers between devices, exchange(): found.append(lax.ppermute(shared, axis, ahead))  9.62 us
    ppermute x4, starting transfers between devices, exchange(): found.append(lax.ppermute(shared, axis, ahead))  9.04 us
    ppermute x4, starting transfers between devices, exchange(): found.append(lax.ppermute(shared, axis, [(b, a) for a, b in ahead]))  6.86 us
  transfers between devices with their start and end apart: 8, of which 3 were waited for; matrix products, arithmetic and copies ran while one was open for 0% of the time, Pallas kernels for 1%

profile of v3, /device:TPU:33, one launch (start us, length us, event | category | flops | bytes accessed | tf_op | source)
XLA Modules:
  0.0 62.2 jit_solution(9351720154135497675)
XLA Ops:
  0.6 1.9 %pick_kernel.1 = (bf16[64,192]{1,0:T(8,128)(2,1)S(1)}, s32[1,64]{1,0:T(1,128)}, bf16[192,512]{1,0:T(8,128)(2,1)S(1)}, s32[1,16]{1,0:T(1,128)S(1)}, f32[1,192]{1,...) custom-call(s32[1,64]{1,0:T(1,128)} %refs_0_.2, ...), custom_call_target="tpu_custom_call" | custom-call | tf_op jit(solution)/shard_map/pick_kernel/pallas_call | solution.py:278
  2.5 0.7 %collective-permute-start.3 = (bf16[64,192]{1,0:T(8,128)(2,1)S(1)}, bf16[64,192]{1,0:T(8,128)(2,1)S(1)}, u32[]{:S(2)}, u32[]{:S(2)}) collective-permute-start(bf16[64,192]{1,0:T(8,128)(2,1)S(1)} %get-tuple-element.48), channel_id=1, source_target_pairs={{1,0},{2,1},{3,2},{4,3},{5,4},{6,5},{7,6},{8,7},{9,8},{10,9},{11,1... | collective-permute-start | bytes 73736 | tf_op jit(solution)/shard_map/ppermute | solution.py:262
  3.2 2.0 %collective-permute-start.2 = (bf16[64,192]{1,0:T(8,128)(2,1)S(1)}, bf16[64,192]{1,0:T(8,128)(2,1)S(1)}, u32[]{:S(2)}, u32[]{:S(2)}) collective-permute-start(bf16[64,192]{1,0:T(8,128)(2,1)S(1)} %get-tuple-element.48), channel_id=1, source_target_pairs={{0,1},{1,2},{2,3},{3,4},{4,5},{5,6},{6,7},{7,8},{8,9},{9,10},{10,1... | collective-permute-start | bytes 73736 | tf_op jit(solution)/shard_map/ppermute | solution.py:261
  5.2 4.3 %collective-permute-start.1 = (bf16[64,192]{1,0:T(8,128)(2,1)S(1)}, bf16[64,192]{1,0:T(8,128)(2,1)S(1)}, u32[]{:S(2)}, u32[]{:S(2)}) collective-permute-start(bf16[64,192]{1,0:T(8,128)(2,1)S(1)} %get-tuple-element.48), channel_id=1, source_target_pairs={{16,0},{32,16},{48,32},{64,48},{80,64},{96,80},{112,96},{128,112},... | collective-permute-start | bytes 73736 | tf_op jit(solution)/shard_map/ppermute | solution.py:262
  9.5 1.9 %collective-permute-start = (bf16[64,192]{1,0:T(8,128)(2,1)S(1)}, bf16[64,192]{1,0:T(8,128)(2,1)S(1)}, u32[]{:S(2)}, u32[]{:S(2)}) collective-permute-start(bf16[64,192]{1,0:T(8,128)(2,1)S(1)} %get-tuple-element.48), channel_id=1, source_target_pairs={{0,16},{16,32},{32,48},{48,64},{64,80},{80,96},{96,112},{112,128},... | collective-permute-start | bytes 73736 | tf_op jit(solution)/shard_map/ppermute | solution.py:261
  11.4 0.3 prepare_kernel.1
  11.7 0.0 collective-permute-done.3.refs_16_
  11.7 0.7 %collective-permute-done.2.refs_15_ = bf16[64,192]{1,0:T(8,128)(2,1)S(1)} collective-permute-done((bf16[64,192]{1,0:T(8,128)(2,1)S(1)}, bf16[64,192]{1,0:T(8,128)(2,1)S(1)}, u32[]{:S(2)}, u32[]{:S(2)}) %collective-permute-start.2) | collective-permute-done | bytes 24608 | tf_op jit(solution)/shard_map/ppermute | solution.py:261
  12.4 0.0 collective-permute-done.1.refs_14_
  12.4 5.1 %collective-permute-done.refs_13_ = bf16[64,192]{1,0:T(8,128)(2,1)S(1)} collective-permute-done((bf16[64,192]{1,0:T(8,128)(2,1)S(1)}, bf16[64,192]{1,0:T(8,128)(2,1)S(1)}, u32[]{:S(2)}, u32[]{:S(2)}) %collective-permute-start) | collective-permute-done | bytes 24608 | tf_op jit(solution)/shard_map/ppermute | solution.py:261
  17.5 5.6 %fine_kernel.1 = (bf16[192,512]{1,0:T(8,128)(2,1)}, bf16[16,104,128]{2,1,0:T(8,128)(2,1)S(1)}, s32[1,384]{1,0:T(1,128)S(1)}, s32[1,384]{1,0:T(1,128)S(1)}, f32[1...) custom-call(s32[1,384]{1,0:T(1,128)} %refs_0_.3, ...), custom_call_target="tpu_custom_call" | custom-call | tf_op jit(solution)/shard_map/fine_kernel/pallas_call | solution.py:278
  23.0 25.7 %all_to_all.5.parts_ref = bf16[16,104,128]{2,1,0:T(8,128)(2,1)S(1)} all-to-all(bf16[16,104,128]{2,1,0:T(8,128)(2,1)S(1)} %get-tuple-element.55), channel_id=1, replica_groups=mesh['px'=32,'py'=16] {'py'}, dimensions={0} | all-to-all | bytes 851968 | tf_op jit(solution)/shard_map/all_to_all | solution.py:393
  48.7 0.2 coarse_kernel.1
  49.0 0.0 collective-permute-start.7
  49.0 1.8 %collective-permute-start.6 = (bf16[16,192]{1,0:T(8,128)(2,1)S(1)}, bf16[16,192]{1,0:T(8,128)(2,1)S(1)}, u32[]{:S(2)}, u32[]{:S(2)}) collective-permute-start(bf16[16,192]{1,0:T(8,128)(2,1)S(1)} %get-tuple-element.70), channel_id=1, source_target_pairs={{0,1},{1,2},{2,3},{3,4},{4,5},{5,6},{6,7},{7,8},{8,9},{9,10},{10,1... | collective-permute-start | bytes 18440 | tf_op jit(solution)/shard_map/ppermute | solution.py:261
  50.7 1.9 %collective-permute-start.5 = (bf16[16,192]{1,0:T(8,128)(2,1)S(1)}, bf16[16,192]{1,0:T(8,128)(2,1)S(1)}, u32[]{:S(2)}, u32[]{:S(2)}) collective-permute-start(bf16[16,192]{1,0:T(8,128)(2,1)S(1)} %get-tuple-element.70), channel_id=1, source_target_pairs={{16,0},{32,16},{48,32},{64,48},{80,64},{96,80},{112,96},{128,112},... | collective-permute-start | bytes 18440 | tf_op jit(solution)/shard_map/ppermute | solution.py:262
  52.6 3.4 %collective-permute-start.4 = (bf16[16,192]{1,0:T(8,128)(2,1)S(1)}, bf16[16,192]{1,0:T(8,128)(2,1)S(1)}, u32[]{:S(2)}, u32[]{:S(2)}) collective-permute-start(bf16[16,192]{1,0:T(8,128)(2,1)S(1)} %get-tuple-element.70), channel_id=1, source_target_pairs={{0,16},{16,32},{32,48},{48,64},{64,80},{80,96},{96,112},{112,128},... | collective-permute-start | bytes 18440 | tf_op jit(solution)/shard_map/ppermute | solution.py:261
  56.0 0.4 prepare3_kernel.1
  56.4 0.0 collective-permute-done.7.h3
  56.5 0.0 collective-permute-done.6.h2
  56.5 0.0 collective-permute-done.5.h1
  56.5 3.9 %collective-permute-done.4.h0 = bf16[16,192]{1,0:T(8,128)(2,1)S(1)} collective-permute-done((bf16[16,192]{1,0:T(8,128)(2,1)S(1)}, bf16[16,192]{1,0:T(8,128)(2,1)S(1)}, u32[]{:S(2)}, u32[]{:S(2)}) %collective-permute-start.4) | collective-permute-done | bytes 6176 | tf_op jit(solution)/shard_map/ppermute | solution.py:261
  60.4 1.8 %level3_kernel.1 = bf16[64,192]{1,0:T(8,128)(2,1)} custom-call(bf16[192,64]{1,0:T(8,128)(2,1)S(1)} %get-tuple-element.57.feat_ref, f32[192,384]{1,0:T(8,128)S(1)} %get-tuple-element.65.half_ref, bf16[64,384]{1,0:T(8,128)(2,1)S(1)} %get-tuple-element.66.around_ref, bf16[64,384]{1,0:T(8,128)(2,1)S(1)} %get-tuple-element.67.target_ref, ...), custom_call_target="tpu_custom_call" | custom-call | tf_op jit(solution)/shard_map/level3_kernel/pallas_call | solution.py:278
Async XLA Ops:
  2.5 9.2 %collective-permute-start.3 = (bf16[64,192]{1,0:T(8,128)(2,1)S(1)}, bf16[64,192]{1,0:T(8,128)(2,1)S(1)}, u32[]{:S(2)}, u32[]{:S(2)}) collective-permute-start(bf16[64,192]{1,0:T(8,128)(2,1)S(1)} %get-tuple-element.48), channel_id=1, source_target_pairs={{1,0},{2,1},{3,2},{4,3},{5,4},{6,5},{7,6},{8,7},{9,8},{10,9},{11,1... | collective-permute-start | bytes 73736 | tf_op jit(solution)/shard_map/ppermute | solution.py:262
  3.2 9.2 %collective-permute-start.2 = (bf16[64,192]{1,0:T(8,128)(2,1)S(1)}, bf16[64,192]{1,0:T(8,128)(2,1)S(1)}, u32[]{:S(2)}, u32[]{:S(2)}) collective-permute-start(bf16[64,192]{1,0:T(8,128)(2,1)S(1)} %get-tuple-element.48), channel_id=1, source_target_pairs={{0,1},{1,2},{2,3},{3,4},{4,5},{5,6},{6,7},{7,8},{8,9},{9,10},{10,1... | collective-permute-start | bytes 73736 | tf_op jit(solution)/shard_map/ppermute | solution.py:261
  5.2 7.2 %collective-permute-start.1 = (bf16[64,192]{1,0:T(8,128)(2,1)S(1)}, bf16[64,192]{1,0:T(8,128)(2,1)S(1)}, u32[]{:S(2)}, u32[]{:S(2)}) collective-permute-start(bf16[64,192]{1,0:T(8,128)(2,1)S(1)} %get-tuple-element.48), channel_id=1, source_target_pairs={{16,0},{32,16},{48,32},{64,48},{80,64},{96,80},{112,96},{128,112},... | collective-permute-start | bytes 73736 | tf_op jit(solution)/shard_map/ppermute | solution.py:262
  9.5 8.0 %collective-permute-start = (bf16[64,192]{1,0:T(8,128)(2,1)S(1)}, bf16[64,192]{1,0:T(8,128)(2,1)S(1)}, u32[]{:S(2)}, u32[]{:S(2)}) collective-permute-start(bf16[64,192]{1,0:T(8,128)(2,1)S(1)} %get-tuple-element.48), channel_id=1, source_target_pairs={{0,16},{16,32},{32,48},{48,64},{64,80},{80,96},{96,112},{112,128},... | collective-permute-start | bytes 73736 | tf_op jit(solution)/shard_map/ppermute | solution.py:261
  49.0 7.5 %collective-permute-start.7 = (bf16[16,192]{1,0:T(8,128)(2,1)S(1)}, bf16[16,192]{1,0:T(8,128)(2,1)S(1)}, u32[]{:S(2)}, u32[]{:S(2)}) collective-permute-start(bf16[16,192]{1,0:T(8,128)(2,1)S(1)} %get-tuple-element.70), channel_id=1, source_target_pairs={{1,0},{2,1},{3,2},{4,3},{5,4},{6,5},{7,6},{8,7},{9,8},{10,9},{11,1... | collective-permute-start | bytes 18440 | tf_op jit(solution)/shard_map/ppermute | solution.py:262
  49.0 7.5 %collective-permute-start.6 = (bf16[16,192]{1,0:T(8,128)(2,1)S(1)}, bf16[16,192]{1,0:T(8,128)(2,1)S(1)}, u32[]{:S(2)}, u32[]{:S(2)}) collective-permute-start(bf16[16,192]{1,0:T(8,128)(2,1)S(1)} %get-tuple-element.70), channel_id=1, source_target_pairs={{0,1},{1,2},{2,3},{3,4},{4,5},{5,6},{6,7},{7,8},{8,9},{9,10},{10,1... | collective-permute-start | bytes 18440 | tf_op jit(solution)/shard_map/ppermute | solution.py:261
  50.7 5.7 %collective-permute-start.5 = (bf16[16,192]{1,0:T(8,128)(2,1)S(1)}, bf16[16,192]{1,0:T(8,128)(2,1)S(1)}, u32[]{:S(2)}, u32[]{:S(2)}) collective-permute-start(bf16[16,192]{1,0:T(8,128)(2,1)S(1)} %get-tuple-element.70), channel_id=1, source_target_pairs={{16,0},{32,16},{48,32},{64,48},{80,64},{96,80},{112,96},{128,112},... | collective-permute-start | bytes 18440 | tf_op jit(solution)/shard_map/ppermute | solution.py:262
  52.6 7.7 %collective-permute-start.4 = (bf16[16,192]{1,0:T(8,128)(2,1)S(1)}, bf16[16,192]{1,0:T(8,128)(2,1)S(1)}, u32[]{:S(2)}, u32[]{:S(2)}) collective-permute-start(bf16[16,192]{1,0:T(8,128)(2,1)S(1)} %get-tuple-element.70), channel_id=1, source_target_pairs={{0,16},{16,32},{32,48},{48,64},{64,80},{80,96},{96,112},{112,128},... | collective-permute-start | bytes 18440 | tf_op jit(solution)/shard_map/ppermute | solution.py:261

commit v4 on v3

--- a/solution.py
+++ b/solution.py
@@ -55,15 +55,13 @@
     return jnp.where(lane == ids, 1.0, 0.0).astype(BF16)
 
 
-def inside_flags():
+def halo_rows(refs):
     i, j = lax.axis_index("px"), lax.axis_index("py")
-    return (i > 0, i < lax.axis_size("px") - 1, j > 0, j < lax.axis_size("py") - 1)
-
-
-def halo_rows(refs):
-    rows = []
-    for ref, inside in zip(refs, inside_flags()):
-        rows.append(jnp.where(inside, ref[...].astype(F32), 0.0).astype(BF16))
+    even, odd, low, high = [ref[...].astype(F32) for ref in refs]
+    is_odd = lax.rem(i, 2) == 1
+    inside = (i > 0, i < lax.axis_size("px") - 1, j > 0, j < lax.axis_size("py") - 1)
+    found = (jnp.where(is_odd, even, odd), jnp.where(is_odd, odd, even), low, high)
+    rows = [jnp.where(flag, part, 0.0).astype(BF16) for flag, part in zip(inside, found)]
     return jnp.concatenate(rows, axis=0)
 
 
@@ -80,21 +78,15 @@
         copy.wait()
 
 
-def prepare_kernel(
-    send3_ref,
-    bias_ref,
-    nbias_ref,
-    wout_ref,
-    nout_ref,
-    feat_ref,
-    win_ref,
-    own_ref,
-    into_ref,
-    cols_ref,
-    wide_ref,
-    chosen_ref,
-):
-    chosen_ref[...] = chooser(send3_ref[...], CLUST_DEV)
+def prepare_kernel(*refs):
+    count = (len(refs) - 7) // 2
+    sources, feat_ref = refs[:count], refs[count]
+    own_ref, into_ref, cols_ref, wide_ref, chosen_ref = refs[count + 1 : count + 6]
+    targets, sems = refs[count + 6 : -1], refs[-1]
+    copies = fetch(sources, targets, sems)
+    win_ref, send3_ref, bias_ref, nbias_ref, wout_ref, nout_ref = targets[:6]
+    for copy in copies[:6]:
+        copy.wait()
     features = feat_ref[...]
     own_ref[...] = (0.5 * nn(win_ref[:, :WIDTH], features)).astype(BF16)
     into_ref[...] = (0.5 * nn(win_ref[:, WIDTH:], features)).astype(BF16)
@@ -102,22 +94,12 @@
     wide_ref[1] = nout_ref[...].astype(F32).T.astype(BF16)
     cols_ref[0] = jnp.broadcast_to(column(0.5 * bias_ref[...], WIDTH), (WIDTH, 128))
     cols_ref[1] = jnp.broadcast_to(column(0.5 * nbias_ref[...], WIDTH), (WIDTH, 128))
-
-
-def fine_kernel(*refs):
-    far = (len(refs) - 22) // 2
-    sources, near, refs = refs[:far], refs[far : far + 15], refs[far + 15 :]
-    (updated_ref, payload_ref), targets, refs = refs[:2], refs[2 : 2 + far], refs[2 + far :]
-    picks_ref, totals_ref, result_ref, sems, result_sem = refs
-    copies = fetch(sources, targets, sems)
-    leave = pltpu.make_async_copy(result_ref, updated_ref, result_sem)
-    fine_round(*near, result_ref, leave, payload_ref, picks_ref, totals_ref)
-    for copy in copies:
+    chosen_ref[...] = chooser(send3_ref[...], CLUST_DEV)
+    for copy in copies[6:]:
         copy.wait()
-    leave.wait()
-
-
-def fine_round(
+
+
+def fine_kernel(
     feat_ref,
     own_ref,
     into_ref,
@@ -134,7 +116,6 @@
     owner_ref,
     member_ref,
     updated_ref,
-    leave,
     payload_ref,
     picks_ref,
     totals_ref,
@@ -164,7 +145,6 @@
     updated = features.astype(F32) + normed(nn(wide_ref[1], half_silu(half).astype(BF16)), 0)
     updated = updated.astype(BF16)
     updated_ref[...] = updated
-    leave.start()
 
     position = owner_ref[...] * CLUST_DEV + member_ref[...]
     counted = jnp.concatenate([updated, jnp.ones((16, nodes), BF16)], axis=0)
@@ -254,13 +234,15 @@
 
 
 def exchange(shared):
-    found = []
-    for axis, closed in (("px", False), ("py", True)):
-        count = lax.axis_size(axis)
-        ahead = [(k, (k + 1) % count) for k in range(count if closed else count - 1)]
-        found.append(lax.ppermute(shared, axis, ahead))
-        found.append(lax.ppermute(shared, axis, [(b, a) for a, b in ahead]))
-    return found
+    count = lax.axis_size("py")
+    ahead = [(k, (k + 1) % count) for k in range(count)]
+    along = [lax.ppermute(shared, "py", ahead)]
+    along.append(lax.ppermute(shared, "py", [(b, a) for a, b in ahead]))
+    across = []
+    for first in (0, 1):
+        pairs = [(k, k + 1) for k in range(first, lax.axis_size("px") - 1, 2)]
+        across.append(lax.ppermute(shared, "px", pairs + [(b, a) for a, b in pairs]))
+    return across + along
 
 
 def fetch(sources, targets, sems):
@@ -313,29 +295,32 @@
     nodes = node_features.shape[0]
     outs = lambda arrays: [(array.shape, array.dtype) for array in arrays]
     dma = pltpu.SemaphoreType.DMA
+    held = (halo_send, node_features.T)
+    shared, _, features = call(
+        pick_kernel,
+        [((halo_send.shape[1], WIDTH), BF16)] + outs(held),
+        [dma((len(held),))],
+        far=held,
+    )
+    rims = exchange(shared)
     held = (
-        halo_send,
-        node_features.T,
+        edge_weight_in.T,
         coarse_send,
         edge_bias[None],
         node_bias[None],
         edge_weight_out,
         node_weight_out,
-        edge_weight_in.T,
         node_weight_in.T,
         edge_source,
         edge_target,
         cluster_owner.reshape(1, nodes),
         cluster_member.reshape(1, nodes),
-    )
-    shared, _, features, send3, bias, nbias, w_out, n_out, w_in, n_in, *ids = call(
-        pick_kernel,
-        [((halo_send.shape[1], WIDTH), BF16)] + outs(held),
-        [dma((len(held),))],
-        far=held,
-    )
-    rims = exchange(shared)
-    own, into, cols, wide, chosen = call(
+        coarse_source,
+        coarse_target,
+        coarse_edge_bias[None],
+        coarse_node_bias[None],
+    )
+    own, into, cols, wide, chosen, *held = call(
         prepare_kernel,
         [
             ((WIDTH, nodes), BF16),
@@ -343,37 +328,17 @@
             ((2, WIDTH, 128), F32),
             ((2, WIDTH, WIDTH), BF16),
             ((coarse_send.shape[1], CLUST_DEV), BF16),
-        ],
-        [],
-        send3,
-        bias,
-        nbias,
-        w_out,
-        n_out,
+        ]
+        + outs(held),
+        [dma((len(held),))],
         features,
-        w_in,
-    )
-    source, target, owner, member = ids
-    far3 = (
-        coarse_source,
-        coarse_target,
-        coarse_edge_bias[None],
-        coarse_node_bias[None],
-        coarse_edge_out,
-        coarse_node_out,
-        coarse_edge_in.T,
-        coarse_node_in.T,
-    )
-    updated, payload, *held3 = call(
+        far=held,
+    )
+    w_in, n_in, source, target, owner, member = held[:1] + held[6:11]
+    updated, payload = call(
         fine_kernel,
-        [((WIDTH, nodes), BF16), ((OWNERS, WIDTH // 2 + 8, 2 * CLUST_DEV), BF16)] + outs(far3),
-        [
-            pltpu.VMEM((WIDTH, 1280), BF16),
-            pltpu.VMEM((WIDTH, nodes), F32),
-            pltpu.VMEM((WIDTH, nodes), BF16),
-            dma((len(far3),)),
-            dma,
-        ],
+        [((WIDTH, nodes), BF16), ((OWNERS, WIDTH // 2 + 8, 2 * CLUST_DEV), BF16)],
+        [pltpu.VMEM((WIDTH, 1280), BF16), pltpu.VMEM((WIDTH, nodes), F32)],
         features,
         own,
         into,
@@ -386,10 +351,8 @@
         n_in,
         owner,
         member,
-        far=far3,
         leave=(0,),
     )
-    w_in3, n_in3 = held3[6:]
     parts = lax.all_to_all(payload, "py", 0, 0, tiled=True)
     coarse, coarse_shared = call(
         coarse_kernel,
@@ -410,9 +373,11 @@
             ((2, WIDTH, WIDTH), BF16),
         ],
         [],
-        *held3[:6],
+        *held[11:],
+        coarse_edge_out,
+        coarse_node_out,
         coarse,
-        w_in3,
+        coarse_edge_in.T,
     )
     (cluster_updated,) = call(
         level3_kernel,
@@ -421,8 +386,8 @@
         coarse,
         *prepared,
         *coarse_rims,
-        w_in3,
-        n_in3,
+        coarse_edge_in.T,
+        coarse_node_in.T,
         leave=(0,),
     )
     return updated.T, cluster_updated

time: 62.5 us -> 57 us (0.912)
  waiting for transfers between devices: 9.63 us -> 2.36 us
  starting transfers between devices: 15.9 us -> 16.9 us
  Pallas kernels: 10.2 us -> 11 us
    ppermute x8, waiting for transfers between devices: 9.63 us -> 2.36 us  [the longest x4 2.35 us: exchange(): lax.ppermute(shared, 'px', pairs + [(b, a) for a, b in pairs])]
    ppermute x8, starting transfers between devices: 15.9 us -> 16.9 us  [the longest x4 12.5 us: exchange(): lax.ppermute(shared, 'px', pairs + [(b, a) for a, b in pairs])]
    pallas_call x6, Pallas kernels: 10.2 us -> 11 us  [call(): pl.pallas_call(kernel, out_shape=[(jax.ShapeDtypeStruct if k in leave els...]
  transfers between devices with their start and end apart: 8 -> 8, of which waited for: 3 -> 3; matrix products, arithmetic and copies ran while one was open for 0% -> 0% of each run, Pallas kernels for 1% -> 5%
where the time goes in v4:
time: 57 us; the launch traced here: 56.7 us
  blocking collectives  25.7 us (45%)
  starting transfers between devices  16.9 us (30%)
  Pallas kernels  11 us (19%)
  waiting for transfers between devices  2.36 us (4%)
  between operations  0.76 us (1%)
    all_to_all x1, blocking collectives, body(): parts = lax.all_to_all(payload, 'py', 0, 0, tiled=True)  25.7 us
    ppermute x4, starting transfers between devices, exchange(): lax.ppermute(shared, 'px', pairs + [(b, a) for a, b in pairs])  12.5 us
    pallas_call x6, Pallas kernels, call(): pl.pallas_call(kernel, out_shape=[(jax.ShapeDtypeStruct if k in leave els...  11 us
    ppermute x2, starting transfers between devices, exchange(): along = [lax.ppermute(shared, 'py', ahead)]  3.76 us
    ppermute x4, waiting for transfers between devices, exchange(): lax.ppermute(shared, 'px', pairs + [(b, a) for a, b in pairs])  2.35 us
  transfers between devices with their start and end apart: 8, of which 3 were waited for; matrix products, arithmetic and copies ran while one was open for 0% of the time, Pallas kernels for 5%

profile of v4, /device:TPU:33, one launch (start us, length us, event | category | flops | bytes accessed | tf_op | source)
XLA Modules:
  0.0 56.7 jit_solution(11476608439001145144)
XLA Ops:
  0.6 1.5 %pick_kernel.1 = (bf16[64,192]{1,0:T(8,128)(2,1)S(1)}, s32[1,64]{1,0:T(1,128)}, bf16[192,512]{1,0:T(8,128)(2,1)S(1)}) custom-call(s32[1,64]{1,0:T(1,128)} %refs_0_.1, bf16[192,512]{1,0:T(8,128)(2,1)} %bitcast.15), custom_call_target="tpu_custom_call" | custom-call | tf_op jit(solution)/shard_map/pick_kernel/pallas_call | solution.py:260
  2.1 0.7 %collective-permute-start.3 = (bf16[64,192]{1,0:T(8,128)(2,1)S(1)}, bf16[64,192]{1,0:T(8,128)(2,1)S(1)}, u32[]{:S(2)}, u32[]{:S(2)}) collective-permute-start(bf16[64,192]{1,0:T(8,128)(2,1)S(1)} %get-tuple-element.33), channel_id=1, source_target_pairs={{1,0},{2,1},{3,2},{4,3},{5,4},{6,5},{7,6},{8,7},{9,8},{10,9},{11,1... | collective-permute-start | bytes 73736 | tf_op jit(solution)/shard_map/ppermute | solution.py:240
  2.8 2.0 %collective-permute-start.2 = (bf16[64,192]{1,0:T(8,128)(2,1)S(1)}, bf16[64,192]{1,0:T(8,128)(2,1)S(1)}, u32[]{:S(2)}, u32[]{:S(2)}) collective-permute-start(bf16[64,192]{1,0:T(8,128)(2,1)S(1)} %get-tuple-element.33), channel_id=1, source_target_pairs={{0,1},{1,2},{2,3},{3,4},{4,5},{5,6},{6,7},{7,8},{8,9},{9,10},{10,1... | collective-permute-start | bytes 73736 | tf_op jit(solution)/shard_map/ppermute | solution.py:239
  4.8 4.3 %collective-permute-start.1 = (bf16[64,192]{1,0:T(8,128)(2,1)S(1)}, bf16[64,192]{1,0:T(8,128)(2,1)S(1)}, u32[]{:S(2)}, u32[]{:S(2)}) collective-permute-start(bf16[64,192]{1,0:T(8,128)(2,1)S(1)} %get-tuple-element.33), channel_id=1, source_target_pairs={{16,32},{48,64},{80,96},{112,128},{144,160},{176,192},{208,224},{2... | collective-permute-start | bytes 73736 | tf_op jit(solution)/shard_map/ppermute | solution.py:244
  9.1 2.0 %collective-permute-start = (bf16[64,192]{1,0:T(8,128)(2,1)S(1)}, bf16[64,192]{1,0:T(8,128)(2,1)S(1)}, u32[]{:S(2)}, u32[]{:S(2)}) collective-permute-start(bf16[64,192]{1,0:T(8,128)(2,1)S(1)} %get-tuple-element.33), channel_id=1, source_target_pairs={{0,16},{32,48},{64,80},{96,112},{128,144},{160,176},{192,208},{224... | collective-permute-start | bytes 73736 | tf_op jit(solution)/shard_map/ppermute | solution.py:244
  11.0 2.3 %prepare_kernel.1 = (bf16[192,512]{1,0:T(8,128)(2,1)S(1)}, bf16[192,512]{1,0:T(8,128)(2,1)S(1)}, f32[2,192,128]{2,1,0:T(8,128)S(1)}, bf16[2,192,192]{2,1,0:T(8,1...) custom-call(bf16[192,384]{1,0:T(8,128)(2,1)} %bitcast.16, ...), custom_call_target="tpu_custom_call" | custom-call | tf_op jit(solution)/shard_map/prepare_kernel/pallas_call | solution.py:260
  13.3 0.0 collective-permute-done.3.h3
  13.3 0.0 collective-permute-done.2.h2
  13.3 0.0 collective-permute-done.1.h1
  13.4 0.4 collective-permute-done.h0
  13.7 4.8 %fine_kernel.1 = (bf16[192,512]{1,0:T(8,128)(2,1)}, bf16[16,104,128]{2,1,0:T(8,128)(2,1)S(1)}) custom-call(bf16[192,512]{1,0:T(8,128)(2,1)S(1)} %get-tuple-element.28.refs_15_.feat_ref, bf16[192,512]{1,0:T(8,128)(2,1)S(1)} %get-tuple-element.29.own_ref, bf16[192,512]{1,0:T(8,128)(2,1)S(1)} %get-tuple-element.30.into_ref, ...), custom_call_target="tpu_custom_call" | custom-call | tf_op jit(solution)/shard_map/fine_kernel/pallas_call | solution.py:260
  18.5 25.7 %all_to_all.5.parts_ref = bf16[16,104,128]{2,1,0:T(8,128)(2,1)S(1)} all-to-all(bf16[16,104,128]{2,1,0:T(8,128)(2,1)S(1)} %get-tuple-element.41), channel_id=1, replica_groups=mesh['px'=32,'py'=16] {'py'}, dimensions={0} | all-to-all | bytes 851968 | tf_op jit(solution)/shard_map/all_to_all | solution.py:356
  44.2 0.0 copy-start
  44.2 0.0 copy-start.2
  44.2 0.0 copy-start.3
  44.2 0.2 coarse_kernel.1
  44.4 0.0 collective-permute-start.7
  44.4 1.8 %collective-permute-start.6 = (bf16[16,192]{1,0:T(8,128)(2,1)S(1)}, bf16[16,192]{1,0:T(8,128)(2,1)S(1)}, u32[]{:S(2)}, u32[]{:S(2)}) collective-permute-start(bf16[16,192]{1,0:T(8,128)(2,1)S(1)} %get-tuple-element.53), channel_id=1, source_target_pairs={{0,1},{1,2},{2,3},{3,4},{4,5},{5,6},{6,7},{7,8},{8,9},{9,10},{10,1... | collective-permute-start | bytes 18440 | tf_op jit(solution)/shard_map/ppermute | solution.py:239
  46.2 4.3 %collective-permute-start.5 = (bf16[16,192]{1,0:T(8,128)(2,1)S(1)}, bf16[16,192]{1,0:T(8,128)(2,1)S(1)}, u32[]{:S(2)}, u32[]{:S(2)}) collective-permute-start(bf16[16,192]{1,0:T(8,128)(2,1)S(1)} %get-tuple-element.53), channel_id=1, source_target_pairs={{16,32},{48,64},{80,96},{112,128},{144,160},{176,192},{208,224},{2... | collective-permute-start | bytes 18440 | tf_op jit(solution)/shard_map/ppermute | solution.py:244
  50.5 1.9 %collective-permute-start.4 = (bf16[16,192]{1,0:T(8,128)(2,1)S(1)}, bf16[16,192]{1,0:T(8,128)(2,1)S(1)}, u32[]{:S(2)}, u32[]{:S(2)}) collective-permute-start(bf16[16,192]{1,0:T(8,128)(2,1)S(1)} %get-tuple-element.53), channel_id=1, source_target_pairs={{0,16},{32,48},{64,80},{96,112},{128,144},{160,176},{192,208},{224... | collective-permute-start | bytes 18440 | tf_op jit(solution)/shard_map/ppermute | solution.py:244
  52.4 0.0 copy-done
  52.4 0.0 copy-done.2
  52.5 0.0 copy-done.3
  52.5 0.0 copy-start.1
  52.5 0.4 prepare3_kernel.1
  52.9 0.0 collective-permute-done.7.h3
  52.9 0.0 collective-permute-done.6.h2
  52.9 1.0 %collective-permute-done.5.h1 = bf16[16,192]{1,0:T(8,128)(2,1)S(1)} collective-permute-done((bf16[16,192]{1,0:T(8,128)(2,1)S(1)}, bf16[16,192]{1,0:T(8,128)(2,1)S(1)}, u32[]{:S(2)}, u32[]{:S(2)}) %collective-permute-start.5) | collective-permute-done | bytes 6176 | tf_op jit(solution)/shard_map/ppermute | solution.py:244
  53.9 1.0 %collective-permute-done.4.h0 = bf16[16,192]{1,0:T(8,128)(2,1)S(1)} collective-permute-done((bf16[16,192]{1,0:T(8,128)(2,1)S(1)}, bf16[16,192]{1,0:T(8,128)(2,1)S(1)}, u32[]{:S(2)}, u32[]{:S(2)}) %collective-permute-start.4) | collective-permute-done | bytes 6176 | tf_op jit(solution)/shard_map/ppermute | solution.py:244
  54.9 0.0 copy-done.1
  54.9 1.8 %level3_kernel.1 = bf16[64,192]{1,0:T(8,128)(2,1)} custom-call(bf16[192,64]{1,0:T(8,128)(2,1)S(1)} %get-tuple-element.43.feat_ref, f32[192,384]{1,0:T(8,128)S(1)} %get-tuple-element.48.half_ref, bf16[64,384]{1,0:T(8,128)(2,1)S(1)} %get-tuple-element.49.around_ref, bf16[64,384]{1,0:T(8,128)(2,1)S(1)} %get-tuple-element.50.target_ref, ...), custom_call_target="tpu_custom_call" | custom-call | tf_op jit(solution)/shard_map/level3_kernel/pallas_call | solution.py:260
Async XLA Ops:
  2.1 11.2 %collective-permute-start.3 = (bf16[64,192]{1,0:T(8,128)(2,1)S(1)}, bf16[64,192]{1,0:T(8,128)(2,1)S(1)}, u32[]{:S(2)}, u32[]{:S(2)}) collective-permute-start(bf16[64,192]{1,0:T(8,128)(2,1)S(1)} %get-tuple-element.33), channel_id=1, source_target_pairs={{1,0},{2,1},{3,2},{4,3},{5,4},{6,5},{7,6},{8,7},{9,8},{10,9},{11,1... | collective-permute-start | bytes 73736 | tf_op jit(solution)/shard_map/ppermute | solution.py:240
  2.8 10.5 %collective-permute-start.2 = (bf16[64,192]{1,0:T(8,128)(2,1)S(1)}, bf16[64,192]{1,0:T(8,128)(2,1)S(1)}, u32[]{:S(2)}, u32[]{:S(2)}) collective-permute-start(bf16[64,192]{1,0:T(8,128)(2,1)S(1)} %get-tuple-element.33), channel_id=1, source_target_pairs={{0,1},{1,2},{2,3},{3,4},{4,5},{5,6},{6,7},{7,8},{8,9},{9,10},{10,1... | collective-permute-start | bytes 73736 | tf_op jit(solution)/shard_map/ppermute | solution.py:239
  4.8 8.6 %collective-permute-start.1 = (bf16[64,192]{1,0:T(8,128)(2,1)S(1)}, bf16[64,192]{1,0:T(8,128)(2,1)S(1)}, u32[]{:S(2)}, u32[]{:S(2)}) collective-permute-start(bf16[64,192]{1,0:T(8,128)(2,1)S(1)} %get-tuple-element.33), channel_id=1, source_target_pairs={{16,32},{48,64},{80,96},{112,128},{144,160},{176,192},{208,224},{2... | collective-permute-start | bytes 73736 | tf_op jit(solution)/shard_map/ppermute | solution.py:244
  9.1 4.7 %collective-permute-start = (bf16[64,192]{1,0:T(8,128)(2,1)S(1)}, bf16[64,192]{1,0:T(8,128)(2,1)S(1)}, u32[]{:S(2)}, u32[]{:S(2)}) collective-permute-start(bf16[64,192]{1,0:T(8,128)(2,1)S(1)} %get-tuple-element.33), channel_id=1, source_target_pairs={{0,16},{32,48},{64,80},{96,112},{128,144},{160,176},{192,208},{224... | collective-permute-start | bytes 73736 | tf_op jit(solution)/shard_map/ppermute | solution.py:244
  44.2 8.3 %copy-start = (bf16[384,192]{0,1:T(8,128)(2,1)S(1)}, bf16[384,192]{0,1:T(8,128)(2,1)}, u32[]{:S(2)}) copy-start(bf16[384,192]{0,1:T(8,128)(2,1)} %param.36) | copy-start | bytes 442372
  44.2 8.3 %copy-start.2 = (bf16[192,192]{1,0:T(8,128)(2,1)S(1)}, bf16[192,192]{1,0:T(8,128)(2,1)}, u32[]{:S(2)}) copy-start(bf16[192,192]{1,0:T(8,128)(2,1)} %wout_ref.1) | copy-start | bytes 221188
  44.2 8.3 %copy-start.3 = (bf16[192,192]{1,0:T(8,128)(2,1)S(1)}, bf16[192,192]{1,0:T(8,128)(2,1)}, u32[]{:S(2)}) copy-start(bf16[192,192]{1,0:T(8,128)(2,1)} %nout_ref.1) | copy-start | bytes 221188
  44.4 8.5 %collective-permute-start.7 = (bf16[16,192]{1,0:T(8,128)(2,1)S(1)}, bf16[16,192]{1,0:T(8,128)(2,1)S(1)}, u32[]{:S(2)}, u32[]{:S(2)}) collective-permute-start(bf16[16,192]{1,0:T(8,128)(2,1)S(1)} %get-tuple-element.53), channel_id=1, source_target_pairs={{1,0},{2,1},{3,2},{4,3},{5,4},{6,5},{7,6},{8,7},{9,8},{10,9},{11,1... | collective-permute-start | bytes 18440 | tf_op jit(solution)/shard_map/ppermute | solution.py:240
  44.4 8.5 %collective-permute-start.6 = (bf16[16,192]{1,0:T(8,128)(2,1)S(1)}, bf16[16,192]{1,0:T(8,128)(2,1)S(1)}, u32[]{:S(2)}, u32[]{:S(2)}) collective-permute-start(bf16[16,192]{1,0:T(8,128)(2,1)S(1)} %get-tuple-element.53), channel_id=1, source_target_pairs={{0,1},{1,2},{2,3},{3,4},{4,5},{5,6},{6,7},{7,8},{8,9},{9,10},{10,1... | collective-permute-start | bytes 18440 | tf_op jit(solution)/shard_map/ppermute | solution.py:239
  46.2 7.7 %collective-permute-start.5 = (bf16[16,192]{1,0:T(8,128)(2,1)S(1)}, bf16[16,192]{1,0:T(8,128)(2,1)S(1)}, u32[]{:S(2)}, u32[]{:S(2)}) collective-permute-start(bf16[16,192]{1,0:T(8,128)(2,1)S(1)} %get-tuple-element.53), channel_id=1, source_target_pairs={{16,32},{48,64},{80,96},{112,128},{144,160},{176,192},{208,224},{2... | collective-permute-start | bytes 18440 | tf_op jit(solution)/shard_map/ppermute | solution.py:244
  50.5 4.4 %collective-permute-start.4 = (bf16[16,192]{1,0:T(8,128)(2,1)S(1)}, bf16[16,192]{1,0:T(8,128)(2,1)S(1)}, u32[]{:S(2)}, u32[]{:S(2)}) collective-permute-start(bf16[16,192]{1,0:T(8,128)(2,1)S(1)} %get-tuple-element.53), channel_id=1, source_target_pairs={{0,16},{32,48},{64,80},{96,112},{128,144},{160,176},{192,208},{224... | collective-permute-start | bytes 18440 | tf_op jit(solution)/shard_map/ppermute | solution.py:244
  52.5 2.4 %copy-start.1 = (bf16[384,192]{0,1:T(8,128)(2,1)S(1)}, bf16[384,192]{0,1:T(8,128)(2,1)}, u32[]{:S(2)}) copy-start(bf16[384,192]{0,1:T(8,128)(2,1)} %param.39) | copy-start | bytes 442372

commit v5 on v4

--- a/solution.py
+++ b/solution.py
@@ -8,7 +8,7 @@
 WIDTH = 192
 CLUST_DEV = 64
 OWNERS = 16
-BLOCK = 1024
+BLOCK, AHEAD = 1024, 3
 F32, BF16, I32, I16 = jnp.float32, jnp.bfloat16, jnp.int32, jnp.int16
 
 
@@ -79,32 +79,36 @@
 
 
 def prepare_kernel(*refs):
-    count = (len(refs) - 7) // 2
-    sources, feat_ref = refs[:count], refs[count]
-    own_ref, into_ref, cols_ref, wide_ref, chosen_ref = refs[count + 1 : count + 6]
-    targets, sems = refs[count + 6 : -1], refs[-1]
+    count = (len(refs) - 10) // 2
+    sources, (feat_ref, win_ref, src_ref, tgt_ref) = refs[:count], refs[count : count + 4]
+    picks_ref, cols_ref, wide_ref, chosen_ref, begun_ref = refs[count + 4 : count + 9]
+    targets, sems = refs[count + 9 : -1], refs[-1]
+    send3_ref, bias_ref, nbias_ref, wout_ref, nout_ref = targets[:5]
     copies = fetch(sources, targets, sems)
-    win_ref, send3_ref, bias_ref, nbias_ref, wout_ref, nout_ref = targets[:6]
-    for copy in copies[:6]:
+    features = feat_ref[...]
+    nodes = features.shape[1]
+    picks_ref[:, :nodes] = (0.5 * nn(win_ref[:, :WIDTH], features)).astype(BF16)
+    picks_ref[:, nodes:] = (0.5 * nn(win_ref[:, WIDTH:], features)).astype(BF16)
+    for step in range(AHEAD):
+        at = pl.ds(step * BLOCK, BLOCK)
+        from_own = one_hot_rows(src_ref[:, at], nodes)
+        to_target = one_hot_rows(tgt_ref[:, at], nodes)
+        begun_ref[:, at] = nn(picks_ref[...], jnp.concatenate([from_own, to_target], axis=0))
+    for copy in copies:
         copy.wait()
-    features = feat_ref[...]
-    own_ref[...] = (0.5 * nn(win_ref[:, :WIDTH], features)).astype(BF16)
-    into_ref[...] = (0.5 * nn(win_ref[:, WIDTH:], features)).astype(BF16)
     wide_ref[0] = wout_ref[...].astype(F32).T.astype(BF16)
     wide_ref[1] = nout_ref[...].astype(F32).T.astype(BF16)
     cols_ref[0] = jnp.broadcast_to(column(0.5 * bias_ref[...], WIDTH), (WIDTH, 128))
     cols_ref[1] = jnp.broadcast_to(column(0.5 * nbias_ref[...], WIDTH), (WIDTH, 128))
     chosen_ref[...] = chooser(send3_ref[...], CLUST_DEV)
-    for copy in copies[6:]:
-        copy.wait()
 
 
 def fine_kernel(
     feat_ref,
-    own_ref,
-    into_ref,
+    made_ref,
     cols_ref,
     wide_ref,
+    begun_ref,
     h0,
     h1,
     h2,
@@ -122,15 +126,19 @@
 ):
     nodes = feat_ref.shape[1]
     rim = halo_rows((h0, h1, h2, h3))
-    lookups = nodes + rim.shape[0]
-    picks_ref[:, :nodes] = own_ref[...]
-    picks_ref[:, nodes:lookups] = (0.5 * nt(win_ref[:, :WIDTH], rim)).astype(BF16)
-    picks_ref[:, lookups:] = into_ref[...]
+    around = (0.5 * nt(win_ref[:, :WIDTH], rim)).astype(BF16)
+    picks_ref[:, : 2 * nodes] = made_ref[...]
+    picks_ref[:, 2 * nodes :] = around
     for step in range(src_ref.shape[1] // BLOCK):
         at = pl.ds(step * BLOCK, BLOCK)
-        from_source = one_hot_rows(src_ref[:, at], lookups)
         to_target = one_hot_rows(tgt_ref[:, at], nodes)
-        half = nn(picks_ref[...], jnp.concatenate([from_source, to_target], axis=0))
+        from_rim = one_hot_rows(src_ref[:, at] - nodes, rim.shape[0])
+        if step < AHEAD:
+            half = begun_ref[:, at] + nn(around, from_rim)
+        else:
+            from_own = one_hot_rows(src_ref[:, at], nodes)
+            chosen = jnp.concatenate([from_own, to_target, from_rim], axis=0)
+            half = nn(picks_ref[...], chosen)
         hidden = half_silu(half + jnp.tile(cols_ref[0], (1, BLOCK // 128))).astype(BF16)
         message = normed(nn(wide_ref[0], hidden), 0).astype(BF16)
         added = nt(message, to_target)
@@ -256,7 +264,7 @@
 
 
 def call(kernel, outs, scratch, *args, far=(), leave=()):
-    held, away = pl.BlockSpec(memory_space=pltpu.VMEM), pl.BlockSpec(memory_space=pl.ANY)
+    held, away = pl.BlockSpec(memory_space=pltpu.VMEM), pl.BlockSpec(memory_space=pltpu.HBM)
     return pl.pallas_call(
         kernel,
         out_shape=[
@@ -265,8 +273,12 @@
         in_specs=[away] * len(far) + [held] * len(args),
         out_specs=[away if far and k in leave else held for k in range(len(outs))],
         scratch_shapes=scratch,
+        compiler_params=pltpu.CompilerParams(vmem_limit_bytes=24 << 20),
         name=kernel.__name__,
-    )(*far, *[pltpu.with_memory_space_constraint(arg, pltpu.VMEM) for arg in args])
+    )(
+        *[pltpu.with_memory_space_constraint(array, pltpu.HBM) for array in far],
+        *[pltpu.with_memory_space_constraint(arg, pltpu.VMEM) for arg in args],
+    )
 
 
 def body(
@@ -295,8 +307,8 @@
     nodes = node_features.shape[0]
     outs = lambda arrays: [(array.shape, array.dtype) for array in arrays]
     dma = pltpu.SemaphoreType.DMA
-    held = (halo_send, node_features.T)
-    shared, _, features = call(
+    held = (halo_send, node_features.T, edge_weight_in.T, edge_source, edge_target)
+    shared, _, features, w_in, source, target = call(
         pick_kernel,
         [((halo_send.shape[1], WIDTH), BF16)] + outs(held),
         [dma((len(held),))],
@@ -304,15 +316,12 @@
     )
     rims = exchange(shared)
     held = (
-        edge_weight_in.T,
         coarse_send,
         edge_bias[None],
         node_bias[None],
         edge_weight_out,
         node_weight_out,
         node_weight_in.T,
-        edge_source,
-        edge_target,
         cluster_owner.reshape(1, nodes),
         cluster_member.reshape(1, nodes),
         coarse_source,
@@ -320,30 +329,33 @@
         coarse_edge_bias[None],
         coarse_node_bias[None],
     )
-    own, into, cols, wide, chosen, *held = call(
+    picks, cols, wide, chosen, begun, *held = call(
         prepare_kernel,
         [
-            ((WIDTH, nodes), BF16),
-            ((WIDTH, nodes), BF16),
+            ((WIDTH, 2 * nodes), BF16),
             ((2, WIDTH, 128), F32),
             ((2, WIDTH, WIDTH), BF16),
             ((coarse_send.shape[1], CLUST_DEV), BF16),
+            ((WIDTH, AHEAD * BLOCK), F32),
         ]
         + outs(held),
         [dma((len(held),))],
         features,
+        w_in,
+        source,
+        target,
         far=held,
     )
-    w_in, n_in, source, target, owner, member = held[:1] + held[6:11]
+    n_in, owner, member = held[5:8]
     updated, payload = call(
         fine_kernel,
         [((WIDTH, nodes), BF16), ((OWNERS, WIDTH // 2 + 8, 2 * CLUST_DEV), BF16)],
         [pltpu.VMEM((WIDTH, 1280), BF16), pltpu.VMEM((WIDTH, nodes), F32)],
         features,
-        own,
-        into,
+        picks,
         cols,
         wide,
+        begun,
         *rims,
         source,
         target,
@@ -373,7 +385,7 @@
             ((2, WIDTH, WIDTH), BF16),
         ],
         [],
-        *held[11:],
+        *held[8:],
         coarse_edge_out,
         coarse_node_out,
         coarse,

time: 57 us -> 57 us (level)
  transfers between devices with their start and end apart: 8 -> 8, of which waited for: 3 -> 2; matrix products, arithmetic and copies ran while one was open for 0% -> 0% of each run, Pallas kernels for 5% -> 6%
where the time goes in v5:
time: 57 us; the launch traced here: 56.7 us
  blocking collectives  25.7 us (45%)
  starting transfers between devices  16.9 us (30%)
  Pallas kernels  11.4 us (20%)
  waiting for transfers between devices  2.01 us (4%)
  between operations  0.79 us (1%)
    all_to_all x1, blocking collectives, body(): parts = lax.all_to_all(payload, 'py', 0, 0, tiled=True)  25.7 us
    ppermute x4, starting transfers between devices, exchange(): lax.ppermute(shared, 'px', pairs + [(b, a) for a, b in pairs])  12.4 us
    pallas_call x6, Pallas kernels, call(): pl.pallas_call(kernel, out_shape=[(jax.ShapeDtypeStruct if k in leave els...  11.4 us
    ppermute x2, starting transfers between devices, exchange(): along = [lax.ppermute(shared, 'py', ahead)]  3.76 us
    ppermute x4, waiting for transfers between devices, exchange(): lax.ppermute(shared, 'px', pairs + [(b, a) for a, b in pairs])  2 us
  transfers between devices with their start and end apart: 8, of which 2 were waited for; matrix products, arithmetic and copies ran while one was open for 0% of the time, Pallas kernels for 6%

profile of v5, /device:TPU:33, one launch (start us, length us, event | category | flops | bytes accessed | tf_op | source)
XLA Modules:
  0.0 56.7 jit_solution(13585911232052733325)
XLA Ops:
  0.6 1.7 %pick_kernel.1 = (bf16[64,192]{1,0:T(8,128)(2,1)S(1)}, s32[1,64]{1,0:T(1,128)}, bf16[192,512]{1,0:T(8,128)(2,1)S(1)}, bf16[192,384]{1,0:T(8,128)(2,1)S(1)}, s32[...) custom-call(s32[1,64]{1,0:T(1,128)} %refs_0_.2, bf16[192,512]{1,0:T(8,128)(2,1)} %bitcast.15, bf16[192,384]{1,0:T(8,128)(2,1)} %bitcast.17, ...), custom_call_target="tpu_custom_call" | custom-call | tf_op jit(solution)/shard_map/pick_kernel/pallas_call | solution.py:268
  2.4 0.7 %collective-permute-start.3 = (bf16[64,192]{1,0:T(8,128)(2,1)S(1)}, bf16[64,192]{1,0:T(8,128)(2,1)S(1)}, u32[]{:S(2)}, u32[]{:S(2)}) collective-permute-start(bf16[64,192]{1,0:T(8,128)(2,1)S(1)} %get-tuple-element.36), channel_id=1, source_target_pairs={{1,0},{2,1},{3,2},{4,3},{5,4},{6,5},{7,6},{8,7},{9,8},{10,9},{11,1... | collective-permute-start | bytes 73736 | tf_op jit(solution)/shard_map/ppermute | solution.py:248
  3.1 2.0 %collective-permute-start.2 = (bf16[64,192]{1,0:T(8,128)(2,1)S(1)}, bf16[64,192]{1,0:T(8,128)(2,1)S(1)}, u32[]{:S(2)}, u32[]{:S(2)}) collective-permute-start(bf16[64,192]{1,0:T(8,128)(2,1)S(1)} %get-tuple-element.36), channel_id=1, source_target_pairs={{0,1},{1,2},{2,3},{3,4},{4,5},{5,6},{6,7},{7,8},{8,9},{9,10},{10,1... | collective-permute-start | bytes 73736 | tf_op jit(solution)/shard_map/ppermute | solution.py:247
  5.1 4.3 %collective-permute-start.1 = (bf16[64,192]{1,0:T(8,128)(2,1)S(1)}, bf16[64,192]{1,0:T(8,128)(2,1)S(1)}, u32[]{:S(2)}, u32[]{:S(2)}) collective-permute-start(bf16[64,192]{1,0:T(8,128)(2,1)S(1)} %get-tuple-element.36), channel_id=1, source_target_pairs={{16,32},{48,64},{80,96},{112,128},{144,160},{176,192},{208,224},{2... | collective-permute-start | bytes 73736 | tf_op jit(solution)/shard_map/ppermute | solution.py:252
  9.3 2.0 %collective-permute-start = (bf16[64,192]{1,0:T(8,128)(2,1)S(1)}, bf16[64,192]{1,0:T(8,128)(2,1)S(1)}, u32[]{:S(2)}, u32[]{:S(2)}) collective-permute-start(bf16[64,192]{1,0:T(8,128)(2,1)S(1)} %get-tuple-element.36), channel_id=1, source_target_pairs={{0,16},{32,48},{64,80},{96,112},{128,144},{160,176},{192,208},{224... | collective-permute-start | bytes 73736 | tf_op jit(solution)/shard_map/ppermute | solution.py:252
  11.3 3.1 %prepare_kernel.1 = (bf16[192,1024]{1,0:T(8,128)(2,1)S(1)}, f32[2,192,128]{2,1,0:T(8,128)S(1)}, bf16[2,192,192]{2,1,0:T(8,128)(2,1)S(1)}, bf16[16,64]{1,0:T(8,12...) custom-call(s32[1,16]{1,0:T(1,128)} %refs_0_.3, ...), custom_call_target="tpu_custom_call" | custom-call | tf_op jit(solution)/shard_map/prepare_kernel/pallas_call | solution.py:268
  14.4 0.0 collective-permute-done.3.h3
  14.4 0.0 collective-permute-done.2.h2
  14.5 0.0 collective-permute-done.1.h1
  14.5 0.0 collective-permute-done.h0
  14.5 0.0 copy-start
  14.5 0.0 copy-start.2
  14.5 0.0 copy-start.3
  14.5 0.0 copy-start.1
  14.5 4.0 %fine_kernel.1 = (bf16[192,512]{1,0:T(8,128)(2,1)}, bf16[16,104,128]{2,1,0:T(8,128)(2,1)S(1)}) custom-call(bf16[192,512]{1,0:T(8,128)(2,1)S(1)} %get-tuple-element.28.refs_12_.feat_ref, bf16[192,1024]{1,0:T(8,128)(2,1)S(1)} %get-tuple-element.32.made_ref, f32[2,192,128]{2,1,0:T(8,128)S(1)} %get-tuple-element.33.cols_ref, ...), custom_call_target="tpu_custom_call" | custom-call | tf_op jit(solution)/shard_map/fine_kernel/pallas_call | solution.py:268
  18.6 25.7 %all_to_all.5.parts_ref = bf16[16,104,128]{2,1,0:T(8,128)(2,1)S(1)} all-to-all(bf16[16,104,128]{2,1,0:T(8,128)(2,1)S(1)} %get-tuple-element.41), channel_id=1, replica_groups=mesh['px'=32,'py'=16] {'py'}, dimensions={0} | all-to-all | bytes 851968 | tf_op jit(solution)/shard_map/all_to_all | solution.py:368
  44.2 0.2 coarse_kernel.1
  44.5 0.0 collective-permute-start.7
  44.5 1.8 %collective-permute-start.6 = (bf16[16,192]{1,0:T(8,128)(2,1)S(1)}, bf16[16,192]{1,0:T(8,128)(2,1)S(1)}, u32[]{:S(2)}, u32[]{:S(2)}) collective-permute-start(bf16[16,192]{1,0:T(8,128)(2,1)S(1)} %get-tuple-element.53), channel_id=1, source_target_pairs={{0,1},{1,2},{2,3},{3,4},{4,5},{5,6},{6,7},{7,8},{8,9},{9,10},{10,1... | collective-permute-start | bytes 18440 | tf_op jit(solution)/shard_map/ppermute | solution.py:247
  46.2 4.3 %collective-permute-start.5 = (bf16[16,192]{1,0:T(8,128)(2,1)S(1)}, bf16[16,192]{1,0:T(8,128)(2,1)S(1)}, u32[]{:S(2)}, u32[]{:S(2)}) collective-permute-start(bf16[16,192]{1,0:T(8,128)(2,1)S(1)} %get-tuple-element.53), channel_id=1, source_target_pairs={{16,32},{48,64},{80,96},{112,128},{144,160},{176,192},{208,224},{2... | collective-permute-start | bytes 18440 | tf_op jit(solution)/shard_map/ppermute | solution.py:252
  50.5 1.9 %collective-permute-start.4 = (bf16[16,192]{1,0:T(8,128)(2,1)S(1)}, bf16[16,192]{1,0:T(8,128)(2,1)S(1)}, u32[]{:S(2)}, u32[]{:S(2)}) collective-permute-start(bf16[16,192]{1,0:T(8,128)(2,1)S(1)} %get-tuple-element.53), channel_id=1, source_target_pairs={{0,16},{32,48},{64,80},{96,112},{128,144},{160,176},{192,208},{224... | collective-permute-start | bytes 18440 | tf_op jit(solution)/shard_map/ppermute | solution.py:252
  52.4 0.0 copy-done
  52.4 0.0 copy-done.2
  52.4 0.0 copy-done.3
  52.5 0.4 prepare3_kernel.1
  52.9 0.0 collective-permute-done.7.h3
  52.9 0.0 collective-permute-done.6.h2
  52.9 1.0 %collective-permute-done.5.h1 = bf16[16,192]{1,0:T(8,128)(2,1)S(1)} collective-permute-done((bf16[16,192]{1,0:T(8,128)(2,1)S(1)}, bf16[16,192]{1,0:T(8,128)(2,1)S(1)}, u32[]{:S(2)}, u32[]{:S(2)}) %collective-permute-start.5) | collective-permute-done | bytes 6176 | tf_op jit(solution)/shard_map/ppermute | solution.py:252
  53.9 1.0 %collective-permute-done.4.h0 = bf16[16,192]{1,0:T(8,128)(2,1)S(1)} collective-permute-done((bf16[16,192]{1,0:T(8,128)(2,1)S(1)}, bf16[16,192]{1,0:T(8,128)(2,1)S(1)}, u32[]{:S(2)}, u32[]{:S(2)}) %collective-permute-start.4) | collective-permute-done | bytes 6176 | tf_op jit(solution)/shard_map/ppermute | solution.py:252
  54.9 0.0 copy-done.1
  54.9 1.8 %level3_kernel.1 = bf16[64,192]{1,0:T(8,128)(2,1)} custom-call(bf16[192,64]{1,0:T(8,128)(2,1)S(1)} %get-tuple-element.43.feat_ref, f32[192,384]{1,0:T(8,128)S(1)} %get-tuple-element.48.half_ref, bf16[64,384]{1,0:T(8,128)(2,1)S(1)} %get-tuple-element.49.around_ref, bf16[64,384]{1,0:T(8,128)(2,1)S(1)} %get-tuple-element.50.target_ref, ...), custom_call_target="tpu_custom_call" | custom-call | tf_op jit(solution)/shard_map/level3_kernel/pallas_call | solution.py:268
Async XLA Ops:
  2.4 12.1 %collective-permute-start.3 = (bf16[64,192]{1,0:T(8,128)(2,1)S(1)}, bf16[64,192]{1,0:T(8,128)(2,1)S(1)}, u32[]{:S(2)}, u32[]{:S(2)}) collective-permute-start(bf16[64,192]{1,0:T(8,128)(2,1)S(1)} %get-tuple-element.36), channel_id=1, source_target_pairs={{1,0},{2,1},{3,2},{4,3},{5,4},{6,5},{7,6},{8,7},{9,8},{10,9},{11,1... | collective-permute-start | bytes 73736 | tf_op jit(solution)/shard_map/ppermute | solution.py:248
  3.1 11.4 %collective-permute-start.2 = (bf16[64,192]{1,0:T(8,128)(2,1)S(1)}, bf16[64,192]{1,0:T(8,128)(2,1)S(1)}, u32[]{:S(2)}, u32[]{:S(2)}) collective-permute-start(bf16[64,192]{1,0:T(8,128)(2,1)S(1)} %get-tuple-element.36), channel_id=1, source_target_pairs={{0,1},{1,2},{2,3},{3,4},{4,5},{5,6},{6,7},{7,8},{8,9},{9,10},{10,1... | collective-permute-start | bytes 73736 | tf_op jit(solution)/shard_map/ppermute | solution.py:247
  5.1 9.4 %collective-permute-start.1 = (bf16[64,192]{1,0:T(8,128)(2,1)S(1)}, bf16[64,192]{1,0:T(8,128)(2,1)S(1)}, u32[]{:S(2)}, u32[]{:S(2)}) collective-permute-start(bf16[64,192]{1,0:T(8,128)(2,1)S(1)} %get-tuple-element.36), channel_id=1, source_target_pairs={{16,32},{48,64},{80,96},{112,128},{144,160},{176,192},{208,224},{2... | collective-permute-start | bytes 73736 | tf_op jit(solution)/shard_map/ppermute | solution.py:252
  9.3 5.1 %collective-permute-start = (bf16[64,192]{1,0:T(8,128)(2,1)S(1)}, bf16[64,192]{1,0:T(8,128)(2,1)S(1)}, u32[]{:S(2)}, u32[]{:S(2)}) collective-permute-start(bf16[64,192]{1,0:T(8,128)(2,1)S(1)} %get-tuple-element.36), channel_id=1, source_target_pairs={{0,16},{32,48},{64,80},{96,112},{128,144},{160,176},{192,208},{224... | collective-permute-start | bytes 73736 | tf_op jit(solution)/shard_map/ppermute | solution.py:252
  14.5 38.0 %copy-start = (bf16[384,192]{0,1:T(8,128)(2,1)S(1)}, bf16[384,192]{0,1:T(8,128)(2,1)}, u32[]{:S(2)}) copy-start(bf16[384,192]{0,1:T(8,128)(2,1)} %param.36) | copy-start | bytes 442372
  14.5 38.0 %copy-start.2 = (bf16[192,192]{1,0:T(8,128)(2,1)S(1)}, bf16[192,192]{1,0:T(8,128)(2,1)}, u32[]{:S(2)}) copy-start(bf16[192,192]{1,0:T(8,128)(2,1)} %wout_ref.1) | copy-start | bytes 221188
  14.5 38.0 %copy-start.3 = (bf16[192,192]{1,0:T(8,128)(2,1)S(1)}, bf16[192,192]{1,0:T(8,128)(2,1)}, u32[]{:S(2)}) copy-start(bf16[192,192]{1,0:T(8,128)(2,1)} %nout_ref.1) | copy-start | bytes 221188
  14.5 40.4 %copy-start.1 = (bf16[384,192]{0,1:T(8,128)(2,1)S(1)}, bf16[384,192]{0,1:T(8,128)(2,1)}, u32[]{:S(2)}) copy-start(bf16[384,192]{0,1:T(8,128)(2,1)} %param.39) | copy-start | bytes 442372
  44.5 8.4 %collective-permute-start.7 = (bf16[16,192]{1,0:T(8,128)(2,1)S(1)}, bf16[16,192]{1,0:T(8,128)(2,1)S(1)}, u32[]{:S(2)}, u32[]{:S(2)}) collective-permute-start(bf16[16,192]{1,0:T(8,128)(2,1)S(1)} %get-tuple-element.53), channel_id=1, source_target_pairs={{1,0},{2,1},{3,2},{4,3},{5,4},{6,5},{7,6},{8,7},{9,8},{10,9},{11,1... | collective-permute-start | bytes 18440 | tf_op jit(solution)/shard_map/ppermute | solution.py:248
  44.5 8.4 %collective-permute-start.6 = (bf16[16,192]{1,0:T(8,128)(2,1)S(1)}, bf16[16,192]{1,0:T(8,128)(2,1)S(1)}, u32[]{:S(2)}, u32[]{:S(2)}) collective-permute-start(bf16[16,192]{1,0:T(8,128)(2,1)S(1)} %get-tuple-element.53), channel_id=1, source_target_pairs={{0,1},{1,2},{2,3},{3,4},{4,5},{5,6},{6,7},{7,8},{8,9},{9,10},{10,1... | collective-permute-start | bytes 18440 | tf_op jit(solution)/shard_map/ppermute | solution.py:247
  46.2 7.7 %collective-permute-start.5 = (bf16[16,192]{1,0:T(8,128)(2,1)S(1)}, bf16[16,192]{1,0:T(8,128)(2,1)S(1)}, u32[]{:S(2)}, u32[]{:S(2)}) collective-permute-start(bf16[16,192]{1,0:T(8,128)(2,1)S(1)} %get-tuple-element.53), channel_id=1, source_target_pairs={{16,32},{48,64},{80,96},{112,128},{144,160},{176,192},{208,224},{2... | collective-permute-start | bytes 18440 | tf_op jit(solution)/shard_map/ppermute | solution.py:252
  50.5 4.4 %collective-permute-start.4 = (bf16[16,192]{1,0:T(8,128)(2,1)S(1)}, bf16[16,192]{1,0:T(8,128)(2,1)S(1)}, u32[]{:S(2)}, u32[]{:S(2)}) collective-permute-start(bf16[16,192]{1,0:T(8,128)(2,1)S(1)} %get-tuple-element.53), channel_id=1, source_target_pairs={{0,16},{32,48},{64,80},{96,112},{128,144},{160,176},{192,208},{224... | collective-permute-start | bytes 18440 | tf_op jit(solution)/shard_map/ppermute | solution.py:252

commit v6 on v4

--- a/solution.py
+++ b/solution.py
@@ -65,17 +65,8 @@
     return jnp.concatenate(rows, axis=0)
 
 
-def pick_kernel(*refs):
-    count = (len(refs) - 2) // 2
-    sources, out_ref, targets, sems = refs[:count], refs[count], refs[count + 1 : -1], refs[-1]
-    copies = fetch(sources, targets, sems)
-    copies[0].wait()
-    copies[1].wait()
-    send_ref, table_ref = targets[:2]
-    chosen = chooser(send_ref[...], table_ref.shape[1])
-    out_ref[...] = nt(chosen, table_ref[...]).astype(BF16)
-    for copy in copies[2:]:
-        copy.wait()
+def pick_kernel(send_ref, table_ref, out_ref):
+    out_ref[...] = nt(chooser(send_ref[...], table_ref.shape[1]), table_ref[...]).astype(BF16)
 
 
 def prepare_kernel(*refs):
@@ -255,7 +246,7 @@
     return copies
 
 
-def call(kernel, outs, scratch, *args, far=(), leave=()):
+def call(kernel, outs, scratch, *args, far=(), leave=(), loose=False):
     held, away = pl.BlockSpec(memory_space=pltpu.VMEM), pl.BlockSpec(memory_space=pl.ANY)
     return pl.pallas_call(
         kernel,
@@ -266,7 +257,7 @@
         out_specs=[away if far and k in leave else held for k in range(len(outs))],
         scratch_shapes=scratch,
         name=kernel.__name__,
-    )(*far, *[pltpu.with_memory_space_constraint(arg, pltpu.VMEM) for arg in args])
+    )(*far, *(args if loose else [pltpu.with_memory_space_constraint(arg, pltpu.VMEM) for arg in args]))
 
 
 def body(
@@ -295,12 +286,14 @@
     nodes = node_features.shape[0]
     outs = lambda arrays: [(array.shape, array.dtype) for array in arrays]
     dma = pltpu.SemaphoreType.DMA
-    held = (halo_send, node_features.T)
-    shared, _, features = call(
+    features = node_features.T
+    (shared,) = call(
         pick_kernel,
-        [((halo_send.shape[1], WIDTH), BF16)] + outs(held),
-        [dma((len(held),))],
-        far=held,
+        [((halo_send.shape[1], WIDTH), BF16)],
+        [],
+        halo_send,
+        features,
+        loose=True,
     )
     rims = exchange(shared)
     held = (
@@ -317,8 +310,6 @@
         cluster_member.reshape(1, nodes),
         coarse_source,
         coarse_target,
-        coarse_edge_bias[None],
-        coarse_node_bias[None],
     )
     own, into, cols, wide, chosen, *held = call(
         prepare_kernel,
@@ -374,6 +365,8 @@
         ],
         [],
         *held[11:],
+        coarse_edge_bias[None],
+        coarse_node_bias[None],
         coarse_edge_out,
         coarse_node_out,
         coarse,

time: 57 us -> 56.8 us (level)
  local copies, waits for them, and re-layouts: 0.02 us -> 0.66 us
  waiting for transfers between devices: 2.36 us -> 1.74 us
    unnamed x8 -> x14, local copies, waits for them, and re-layouts: 0.02 us -> 0.66 us
    ppermute x4, waiting for transfers between devices: 2.35 us -> 1.73 us  [exchange(): lax.ppermute(shared, 'px', pairs + [(b, a) for a, b in pairs])]
where the time goes in v6:
time: 56.8 us; the launch traced here: 56.5 us
  blocking collectives  25.7 us (45%)
  starting transfers between devices  16.9 us (30%)
  Pallas kernels  10.7 us (19%)
  waiting for transfers between devices  1.74 us (3%)
  between operations  0.78 us (1%)
  local copies, waits for them, and re-layouts  0.66 us (1%)
    all_to_all x1, blocking collectives, body(): parts = lax.all_to_all(payload, 'py', 0, 0, tiled=True)  25.7 us
    ppermute x4, starting transfers between devices, exchange(): lax.ppermute(shared, 'px', pairs + [(b, a) for a, b in pairs])  12.5 us
    pallas_call x6, Pallas kernels, call(): pl.pallas_call(kernel, out_shape=[(jax.ShapeDtypeStruct if k in leave els...  10.7 us
    ppermute x2, starting transfers between devices, exchange(): along = [lax.ppermute(shared, 'py', ahead)]  3.76 us
    ppermute x4, waiting for transfers between devices, exchange(): lax.ppermute(shared, 'px', pairs + [(b, a) for a, b in pairs])  1.73 us
  transfers between devices with their start and end apart: 8, of which 3 were waited for; matrix products, arithmetic and copies ran while one was open for 0% of the time, Pallas kernels for 5%

profile of v6, /device:TPU:33, one launch (start us, length us, event | category | flops | bytes accessed | tf_op | source)
XLA Modules:
  0.0 56.5 jit_solution(15868529460813797501)
XLA Ops:
  0.6 0.0 copy-start
  0.6 1.2 %pick_kernel.1 = bf16[64,192]{1,0:T(8,128)(2,1)S(1)} custom-call(s32[1,64]{1,0:T(1,128)} %send_ref.1, bf16[192,512]{1,0:T(8,128)(2,1)} %bitcast.12), custom_call_target="tpu_custom_call" | custom-call | tf_op jit(solution)/shard_map/pick_kernel/pallas_call | solution.py:251
  1.8 0.7 %collective-permute-start.3 = (bf16[64,192]{1,0:T(8,128)(2,1)S(1)}, bf16[64,192]{1,0:T(8,128)(2,1)S(1)}, u32[]{:S(2)}, u32[]{:S(2)}) collective-permute-start(bf16[64,192]{1,0:T(8,128)(2,1)S(1)} %pick_kernel.1), channel_id=1, source_target_pairs={{1,0},{2,1},{3,2},{4,3},{5,4},{6,5},{7,6},{8,7},{9,8},{10,9},{11,1... | collective-permute-start | bytes 73736 | tf_op jit(solution)/shard_map/ppermute | solution.py:231
  2.5 2.0 %collective-permute-start.2 = (bf16[64,192]{1,0:T(8,128)(2,1)S(1)}, bf16[64,192]{1,0:T(8,128)(2,1)S(1)}, u32[]{:S(2)}, u32[]{:S(2)}) collective-permute-start(bf16[64,192]{1,0:T(8,128)(2,1)S(1)} %pick_kernel.1), channel_id=1, source_target_pairs={{0,1},{1,2},{2,3},{3,4},{4,5},{5,6},{6,7},{7,8},{8,9},{9,10},{10,1... | collective-permute-start | bytes 73736 | tf_op jit(solution)/shard_map/ppermute | solution.py:230
  4.5 4.3 %collective-permute-start.1 = (bf16[64,192]{1,0:T(8,128)(2,1)S(1)}, bf16[64,192]{1,0:T(8,128)(2,1)S(1)}, u32[]{:S(2)}, u32[]{:S(2)}) collective-permute-start(bf16[64,192]{1,0:T(8,128)(2,1)S(1)} %pick_kernel.1), channel_id=1, source_target_pairs={{16,32},{48,64},{80,96},{112,128},{144,160},{176,192},{208,224},{2... | collective-permute-start | bytes 73736 | tf_op jit(solution)/shard_map/ppermute | solution.py:235
  8.8 2.0 %collective-permute-start = (bf16[64,192]{1,0:T(8,128)(2,1)S(1)}, bf16[64,192]{1,0:T(8,128)(2,1)S(1)}, u32[]{:S(2)}, u32[]{:S(2)}) collective-permute-start(bf16[64,192]{1,0:T(8,128)(2,1)S(1)} %pick_kernel.1), channel_id=1, source_target_pairs={{0,16},{32,48},{64,80},{96,112},{128,144},{160,176},{192,208},{224... | collective-permute-start | bytes 73736 | tf_op jit(solution)/shard_map/ppermute | solution.py:235
  10.8 0.0 copy-done
  10.8 2.2 %prepare_kernel.1 = (bf16[192,512]{1,0:T(8,128)(2,1)S(1)}, bf16[192,512]{1,0:T(8,128)(2,1)S(1)}, f32[2,192,128]{2,1,0:T(8,128)S(1)}, bf16[2,192,192]{2,1,0:T(8,1...) custom-call(bf16[192,384]{1,0:T(8,128)(2,1)} %bitcast.20, ...), custom_call_target="tpu_custom_call" | custom-call | tf_op jit(solution)/shard_map/prepare_kernel/pallas_call | solution.py:251
  13.0 0.0 collective-permute-done.3.h3
  13.1 0.0 collective-permute-done.2.h2
  13.1 0.0 collective-permute-done.1.h1
  13.1 0.4 collective-permute-done.h0
  13.5 4.8 %fine_kernel.1 = (bf16[192,512]{1,0:T(8,128)(2,1)}, bf16[16,104,128]{2,1,0:T(8,128)(2,1)S(1)}) custom-call(bf16[192,512]{1,0:T(8,128)(2,1)S(1)} %bitcast.14, bf16[192,512]{1,0:T(8,128)(2,1)S(1)} %get-tuple-element.24.own_ref, bf16[192,512]{1,0:T(8,128)(2,1)S(1)} %get-tuple-element.25.into_ref, f32[2,192,128]{2,1,0:T(8,128)S(1)} %get-tuple-element.26.cols_ref, ...), custom_call_target="tpu_custom_call" | custom-call | tf_op jit(solution)/shard_map/fine_kernel/pallas_call | solution.py:251
  18.2 25.7 %all_to_all.5.parts_ref = bf16[16,104,128]{2,1,0:T(8,128)(2,1)S(1)} all-to-all(bf16[16,104,128]{2,1,0:T(8,128)(2,1)S(1)} %get-tuple-element.35), channel_id=1, replica_groups=mesh['px'=32,'py'=16] {'py'}, dimensions={0} | all-to-all | bytes 851968 | tf_op jit(solution)/shard_map/all_to_all | solution.py:347
  43.9 0.0 copy-start.1
  43.9 0.0 copy-start.3
  43.9 0.0 copy-start.4
  43.9 0.0 copy-start.6
  43.9 0.2 coarse_kernel.1
  44.2 0.0 collective-permute-start.7
  44.2 1.8 %collective-permute-start.6 = (bf16[16,192]{1,0:T(8,128)(2,1)S(1)}, bf16[16,192]{1,0:T(8,128)(2,1)S(1)}, u32[]{:S(2)}, u32[]{:S(2)}) collective-permute-start(bf16[16,192]{1,0:T(8,128)(2,1)S(1)} %get-tuple-element.45), channel_id=1, source_target_pairs={{0,1},{1,2},{2,3},{3,4},{4,5},{5,6},{6,7},{7,8},{8,9},{9,10},{10,1... | collective-permute-start | bytes 18440 | tf_op jit(solution)/shard_map/ppermute | solution.py:230
  45.9 4.3 %collective-permute-start.5 = (bf16[16,192]{1,0:T(8,128)(2,1)S(1)}, bf16[16,192]{1,0:T(8,128)(2,1)S(1)}, u32[]{:S(2)}, u32[]{:S(2)}) collective-permute-start(bf16[16,192]{1,0:T(8,128)(2,1)S(1)} %get-tuple-element.45), channel_id=1, source_target_pairs={{16,32},{48,64},{80,96},{112,128},{144,160},{176,192},{208,224},{2... | collective-permute-start | bytes 18440 | tf_op jit(solution)/shard_map/ppermute | solution.py:235
  50.3 1.9 %collective-permute-start.4 = (bf16[16,192]{1,0:T(8,128)(2,1)S(1)}, bf16[16,192]{1,0:T(8,128)(2,1)S(1)}, u32[]{:S(2)}, u32[]{:S(2)}) collective-permute-start(bf16[16,192]{1,0:T(8,128)(2,1)S(1)} %get-tuple-element.45), channel_id=1, source_target_pairs={{0,16},{32,48},{64,80},{96,112},{128,144},{160,176},{192,208},{224... | collective-permute-start | bytes 18440 | tf_op jit(solution)/shard_map/ppermute | solution.py:235
  52.2 0.0 copy-start.5
  52.2 0.0 copy-done.1
  52.2 0.0 copy-done.3
  52.2 0.0 copy-done.4
  52.2 0.0 copy-done.6
  52.2 0.6 %copy-done.5 = f32[192]{0:T(256)S(1)} copy-done((f32[192]{0:T(256)S(1)}, f32[192]{0:T(256)}, u32[]{:S(2)}) %copy-start.5) | copy-done | bytes 792
  52.9 0.0 copy-start.2
  52.9 0.4 prepare3_kernel.1
  53.3 0.0 collective-permute-done.7.h3
  53.3 0.0 collective-permute-done.6.h2
  53.3 0.3 collective-permute-done.5.h1
  53.6 1.0 %collective-permute-done.4.h0 = bf16[16,192]{1,0:T(8,128)(2,1)S(1)} collective-permute-done((bf16[16,192]{1,0:T(8,128)(2,1)S(1)}, bf16[16,192]{1,0:T(8,128)(2,1)S(1)}, u32[]{:S(2)}, u32[]{:S(2)}) %collective-permute-start.4) | collective-permute-done | bytes 6176 | tf_op jit(solution)/shard_map/ppermute | solution.py:235
  54.7 0.0 copy-done.2
  54.7 1.8 %level3_kernel.1 = bf16[64,192]{1,0:T(8,128)(2,1)} custom-call(bf16[192,64]{1,0:T(8,128)(2,1)S(1)} %get-tuple-element.37.feat_ref, f32[192,384]{1,0:T(8,128)S(1)} %get-tuple-element.40.half_ref, bf16[64,384]{1,0:T(8,128)(2,1)S(1)} %get-tuple-element.41.around_ref, bf16[64,384]{1,0:T(8,128)(2,1)S(1)} %get-tuple-element.42.target_ref, ...), custom_call_target="tpu_custom_call" | custom-call | tf_op jit(solution)/shard_map/level3_kernel/pallas_call | solution.py:251
Async XLA Ops:
  0.6 10.2 %copy-start = (bf16[512,192]{0,1:T(8,128)(2,1)S(1)}, bf16[512,192]{0,1:T(8,128)(2,1)}, u32[]{:S(2)}) copy-start(bf16[512,192]{0,1:T(8,128)(2,1)} %param.21) | copy-start | bytes 589828
  1.8 11.2 %collective-permute-start.3 = (bf16[64,192]{1,0:T(8,128)(2,1)S(1)}, bf16[64,192]{1,0:T(8,128)(2,1)S(1)}, u32[]{:S(2)}, u32[]{:S(2)}) collective-permute-start(bf16[64,192]{1,0:T(8,128)(2,1)S(1)} %pick_kernel.1), channel_id=1, source_target_pairs={{1,0},{2,1},{3,2},{4,3},{5,4},{6,5},{7,6},{8,7},{9,8},{10,9},{11,1... | collective-permute-start | bytes 73736 | tf_op jit(solution)/shard_map/ppermute | solution.py:231
  2.5 10.5 %collective-permute-start.2 = (bf16[64,192]{1,0:T(8,128)(2,1)S(1)}, bf16[64,192]{1,0:T(8,128)(2,1)S(1)}, u32[]{:S(2)}, u32[]{:S(2)}) collective-permute-start(bf16[64,192]{1,0:T(8,128)(2,1)S(1)} %pick_kernel.1), channel_id=1, source_target_pairs={{0,1},{1,2},{2,3},{3,4},{4,5},{5,6},{6,7},{7,8},{8,9},{9,10},{10,1... | collective-permute-start | bytes 73736 | tf_op jit(solution)/shard_map/ppermute | solution.py:230
  4.5 8.5 %collective-permute-start.1 = (bf16[64,192]{1,0:T(8,128)(2,1)S(1)}, bf16[64,192]{1,0:T(8,128)(2,1)S(1)}, u32[]{:S(2)}, u32[]{:S(2)}) collective-permute-start(bf16[64,192]{1,0:T(8,128)(2,1)S(1)} %pick_kernel.1), channel_id=1, source_target_pairs={{16,32},{48,64},{80,96},{112,128},{144,160},{176,192},{208,224},{2... | collective-permute-start | bytes 73736 | tf_op jit(solution)/shard_map/ppermute | solution.py:235
  8.8 4.7 %collective-permute-start = (bf16[64,192]{1,0:T(8,128)(2,1)S(1)}, bf16[64,192]{1,0:T(8,128)(2,1)S(1)}, u32[]{:S(2)}, u32[]{:S(2)}) collective-permute-start(bf16[64,192]{1,0:T(8,128)(2,1)S(1)} %pick_kernel.1), channel_id=1, source_target_pairs={{0,16},{32,48},{64,80},{96,112},{128,144},{160,176},{192,208},{224... | collective-permute-start | bytes 73736 | tf_op jit(solution)/shard_map/ppermute | solution.py:235
  43.9 8.3 %copy-start.1 = (bf16[384,192]{0,1:T(8,128)(2,1)S(1)}, bf16[384,192]{0,1:T(8,128)(2,1)}, u32[]{:S(2)}) copy-start(bf16[384,192]{0,1:T(8,128)(2,1)} %param.36) | copy-start | bytes 442372
  43.9 8.3 %copy-start.3 = (bf16[192,192]{1,0:T(8,128)(2,1)S(1)}, bf16[192,192]{1,0:T(8,128)(2,1)}, u32[]{:S(2)}) copy-start(bf16[192,192]{1,0:T(8,128)(2,1)} %wout_ref.1) | copy-start | bytes 221188
  43.9 8.3 %copy-start.4 = (bf16[192,192]{1,0:T(8,128)(2,1)S(1)}, bf16[192,192]{1,0:T(8,128)(2,1)}, u32[]{:S(2)}) copy-start(bf16[192,192]{1,0:T(8,128)(2,1)} %nout_ref.1) | copy-start | bytes 221188
  43.9 8.3 %copy-start.6 = (f32[192]{0:T(256)S(1)}, f32[192]{0:T(256)}, u32[]{:S(2)}) copy-start(f32[192]{0:T(256)} %param.40) | copy-start | bytes 2308
  44.2 9.1 %collective-permute-start.7 = (bf16[16,192]{1,0:T(8,128)(2,1)S(1)}, bf16[16,192]{1,0:T(8,128)(2,1)S(1)}, u32[]{:S(2)}, u32[]{:S(2)}) collective-permute-start(bf16[16,192]{1,0:T(8,128)(2,1)S(1)} %get-tuple-element.45), channel_id=1, source_target_pairs={{1,0},{2,1},{3,2},{4,3},{5,4},{6,5},{7,6},{8,7},{9,8},{10,9},{11,1... | collective-permute-start | bytes 18440 | tf_op jit(solution)/shard_map/ppermute | solution.py:231
  44.2 9.1 %collective-permute-start.6 = (bf16[16,192]{1,0:T(8,128)(2,1)S(1)}, bf16[16,192]{1,0:T(8,128)(2,1)S(1)}, u32[]{:S(2)}, u32[]{:S(2)}) collective-permute-start(bf16[16,192]{1,0:T(8,128)(2,1)S(1)} %get-tuple-element.45), channel_id=1, source_target_pairs={{0,1},{1,2},{2,3},{3,4},{4,5},{5,6},{6,7},{7,8},{8,9},{9,10},{10,1... | collective-permute-start | bytes 18440 | tf_op jit(solution)/shard_map/ppermute | solution.py:230
  45.9 7.7 %collective-permute-start.5 = (bf16[16,192]{1,0:T(8,128)(2,1)S(1)}, bf16[16,192]{1,0:T(8,128)(2,1)S(1)}, u32[]{:S(2)}, u32[]{:S(2)}) collective-permute-start(bf16[16,192]{1,0:T(8,128)(2,1)S(1)} %get-tuple-element.45), channel_id=1, source_target_pairs={{16,32},{48,64},{80,96},{112,128},{144,160},{176,192},{208,224},{2... | collective-permute-start | bytes 18440 | tf_op jit(solution)/shard_map/ppermute | solution.py:235
  50.3 4.4 %collective-permute-start.4 = (bf16[16,192]{1,0:T(8,128)(2,1)S(1)}, bf16[16,192]{1,0:T(8,128)(2,1)S(1)}, u32[]{:S(2)}, u32[]{:S(2)}) collective-permute-start(bf16[16,192]{1,0:T(8,128)(2,1)S(1)} %get-tuple-element.45), channel_id=1, source_target_pairs={{0,16},{32,48},{64,80},{96,112},{128,144},{160,176},{192,208},{224... | collective-permute-start | bytes 18440 | tf_op jit(solution)/shard_map/ppermute | solution.py:235
  52.2 0.7 %copy-start.5 = (f32[192]{0:T(256)S(1)}, f32[192]{0:T(256)}, u32[]{:S(2)}) copy-start(f32[192]{0:T(256)} %param.37) | copy-start | bytes 2308
  52.9 1.8 %copy-start.2 = (bf16[384,192]{0,1:T(8,128)(2,1)S(1)}, bf16[384,192]{0,1:T(8,128)(2,1)}, u32[]{:S(2)}) copy-start(bf16[384,192]{0,1:T(8,128)(2,1)} %param.39) | copy-start | bytes 442372
